TPU v7x, 256 devices: a whole 4x4x8 slice. The times are simulated.
256 devices in a mesh: strip: 16 (over z, core), sample: 16 (over y, x).
Axes of the slice: x: 4, y: 4, z: 8, core: 2. Of those that a mesh axis runs over, the one named last changes fastest.
Arguments:
- images: bfloat16 [16, 48, 108, 2048], P('sample', 'strip'), may hold values from -36 to 36
- w_point: bfloat16 [2048, 256], P('sample'), may hold values from -0.125 to 0.125
- w_atrous: bfloat16 [2048, 2304], P('sample'), may hold values from -0.046875 to 0.046875
- w_image: bfloat16 [2048, 256], P('sample'), may hold values from -0.125 to 0.125
- w_proj: bfloat16 [768, 256], P('sample'), may hold values from -0.21875 to 0.21875
- cotangent: bfloat16 [16, 48, 108, 256], P('sample', 'strip'), may hold values from -6 to 6
Outputs:
- result: bfloat16 [16, 48, 108, 256], P('sample', 'strip')
- input_grad: bfloat16 [16, 48, 108, 2048], P('sample', 'strip')
- grad_point: float32 [2048, 256], P('sample')
- grad_atrous: float32 [2048, 2304], P('sample')
- grad_image: float32 [2048, 256], P('sample')
- grad_proj: float32 [768, 256], P('sample')
All inputs are finite; a program needn't handle non-finite values.
Results may differ from a plain program's by a relative error of at most 0.038.
Values may be sent and summed in bfloat16 or wider, within the bound.
A program may use at most 128 MiB of HBM per device.

v0:
```python
import jax
import jax.numpy as jnp
from jax import lax
from jax.sharding import Mesh
from jax.sharding import PartitionSpec as P

DILATION_RATE = 12
STRIP_SAMPLE = ("strip_0", "strip_1", "sample_0", "sample_1")
STRIP = ("strip_0", "strip_1")
SAMPLE = ("sample_0", "sample_1")


EPSILON = 1e-05


def one_axis_at_a_time(array, axes):
    for axis in axes:
        array = lax.psum(array, axis)
    return array


def side_by_side(arrays, axis, dim, along):
    widths = [a.shape[along] for a in arrays]
    both = jnp.concatenate(arrays, axis=along)
    filled = lax.all_gather(both, axis, axis=dim, tiled=True)
    return tuple(jnp.split(filled, [sum(widths[:k]) for k in range(1, len(widths))], axis=along))


def from_everyone(array, axis):
    peers = lax.axis_size(axis)
    return lax.all_to_all(
        jnp.broadcast_to(array[None], (peers, *array.shape)), axis, 0, 0, tiled=True
    )


def taken_together(array, axis):
    return from_everyone(array, axis).sum(axis=0)


def passed_along(array, axis, by):
    peers = lax.axis_size(axis)
    pairs = [(i, i + by) for i in range(peers) if 0 <= i + by < peers]
    return lax.ppermute(array, axis, pairs)


def cut_along(array, dim, peers):
    before, after = (array.shape[:dim], array.shape[dim + 1 :])
    return jnp.moveaxis(array.reshape(*before, peers, -1, *after), dim, 0)


def sum_at_owner(array, axis, dim):
    tiles = cut_along(array, dim, lax.axis_size(axis))
    arrived = lax.all_to_all(tiles, axis, split_axis=0, concat_axis=0, tiled=True)
    return arrived.astype(jnp.float32).sum(axis=0)


def joined_along(tiles, dim):
    lengths = list(tiles.shape[1:])
    lengths[dim] *= tiles.shape[0]
    return jnp.moveaxis(tiles, 0, dim).reshape(lengths)


def gather_directly(array, axis, dim):
    tiles = from_everyone(array, axis)
    return joined_along(tiles, dim)


def total_of_pieces(array, axis):
    return lax.all_gather(array, axis).astype(jnp.float32).sum(0)


def shifted_axis(values, offset, axis_dim):
    if offset == 0:
        return values
    length = values.shape[axis_dim]
    margin = abs(offset)
    pad_widths = [(0, 0)] * values.ndim
    pad_widths[axis_dim] = (margin, margin)
    padded = jnp.pad(values, pad_widths)
    return lax.slice_in_dim(padded, margin + offset, margin + offset + length, axis=axis_dim)


def contract_last(left, right):
    return lax.dot_general(
        left, right, (((left.ndim - 1,), (1,)), ((), ())), preferred_element_type=jnp.float32
    )


def swish(values):
    return values * jax.nn.sigmoid(values)


def swish_slope(values):
    sigma = jax.nn.sigmoid(values)
    return sigma * (1.0 + values * (1.0 - sigma))


def row_part(source, tap_rows, out_width):
    tap_product = jnp.dot(source, tap_rows, preferred_element_type=jnp.float32)
    summed_terms = jnp.zeros(tap_product.shape[:-1] + (out_width,), jnp.float32)
    for column_stride in (-1, 0, 1):
        kernel_tap_slice = tap_product[
            ..., (column_stride + 1) * out_width : (column_stride + 2) * out_width
        ]
        summed_terms = summed_terms + shifted_axis(
            kernel_tap_slice, DILATION_RATE * column_stride, 1
        )
    return summed_terms


def column_stack(gradient_list):
    return jnp.concatenate(
        [
            shifted_axis(gradient_list, -DILATION_RATE * column_stride, 1)
            for column_stride in (-1, 0, 1)
        ],
        -1,
    )


def moments(values, position_count):
    branch_sums = jnp.stack([jnp.sum(tensor, axis=(0, 1)) for tensor in values])
    squares = jnp.stack([jnp.sum(jnp.square(tensor), axis=(0, 1)) for tensor in values])
    totals, powers = (
        one_axis_at_a_time(branch_sums, STRIP_SAMPLE),
        one_axis_at_a_time(squares, STRIP_SAMPLE),
    )
    centres = totals / position_count
    variances = powers / position_count - jnp.square(centres)
    return (centres, variances)


def on_device(images, w_point, w_atrous, w_image, w_proj, cotangent):
    sample_map = images[0]
    strip_row_count, col_count, chan_count = sample_map.shape
    out_width = w_point.shape[1]
    tap_band = 3 * out_width
    strips = lax.axis_size(STRIP)
    samples = lax.axis_size(SAMPLE)
    map_area = strips * strip_row_count * col_count
    position_count = samples * map_area
    strip_extent = DILATION_RATE // strip_row_count
    factor = 1.0 / samples
    point_full, atrous_full, image_full, proj_full = (
        *side_by_side((w_point, w_atrous, w_image), SAMPLE, 0, 1),
        lax.all_gather(w_proj, SAMPLE, axis=0, tiled=True),
    )
    pool_total = taken_together(jnp.sum(sample_map, axis=(0, 1), dtype=jnp.float32), STRIP)
    pooled = (pool_total / map_area).astype(jnp.bfloat16)

    def tap_rows(row_stride):
        return atrous_full[:, (row_stride + 1) * tap_band : (row_stride + 2) * tap_band]

    point_out = jnp.dot(sample_map, point_full, preferred_element_type=jnp.float32)
    dilated_branch_output = row_part(sample_map, tap_rows(0), out_width)
    for row_stride in (1, -1):
        remote = passed_along(sample_map, STRIP, -row_stride * strip_extent)
        dilated_branch_output = dilated_branch_output + row_part(
            remote, tap_rows(row_stride), out_width
        )
    centres, variances = moments([point_out, dilated_branch_output], position_count)
    scales = lax.rsqrt(variances + EPSILON)
    norm_point = (point_out - centres[0]) * scales[0]
    norm_atrous = (dilated_branch_output - centres[1]) * scales[1]
    relu_joined = jnp.concatenate(
        [swish(norm_point).astype(jnp.bfloat16), swish(norm_atrous).astype(jnp.bfloat16)], -1
    )
    image_out = jnp.dot(pooled, image_full, preferred_element_type=jnp.float32)
    layer_mean = jnp.mean(image_out)
    layer_spread = jnp.mean(jnp.square(image_out - layer_mean))
    layer_scale = lax.rsqrt(layer_spread + EPSILON)
    layer_norm = (image_out - layer_mean) * layer_scale
    relu_image = swish(layer_norm).astype(jnp.bfloat16)
    mixed_out = jnp.dot(relu_joined, proj_full[: 2 * out_width], preferred_element_type=jnp.float32)
    mixed_out = mixed_out + jnp.dot(
        relu_image, proj_full[2 * out_width :], preferred_element_type=jnp.float32
    )
    mix_centre, mix_spread = moments([mixed_out], position_count)
    mix_scale = lax.rsqrt(mix_spread[0] + EPSILON)
    norm_mix = (mixed_out - mix_centre[0]) * mix_scale
    result = swish(norm_mix).astype(jnp.bfloat16)
    upstream = cotangent[0].astype(jnp.float32) * swish_slope(norm_mix)
    first_sum, second_sum = (
        one_axis_at_a_time(jnp.sum(upstream, axis=(0, 1)), STRIP_SAMPLE),
        one_axis_at_a_time(jnp.sum(upstream * norm_mix, axis=(0, 1)), STRIP_SAMPLE),
    )
    grad_mix = (
        upstream - first_sum / position_count - norm_mix * (second_sum / position_count)
    ) * mix_scale
    grad_mix_b = grad_mix.astype(jnp.bfloat16)
    column_total = taken_together(jnp.sum(grad_mix, axis=(0, 1)), STRIP)
    column_b = column_total.astype(jnp.bfloat16)
    back_joined = contract_last(grad_mix_b, proj_full[: 2 * out_width])
    back_image = contract_last(column_b, proj_full[2 * out_width :])
    up_image = back_image * swish_slope(layer_norm)
    grad_image_b = (
        (up_image - jnp.mean(up_image) - layer_norm * jnp.mean(up_image * layer_norm)) * layer_scale
    ).astype(jnp.bfloat16)
    grad_pool = contract_last(grad_image_b, image_full)
    up_point = back_joined[..., :out_width] * swish_slope(norm_point)
    up_atrous = back_joined[..., out_width:] * swish_slope(norm_atrous)
    local_sums = jnp.stack(
        [
            jnp.sum(up_point, axis=(0, 1)),
            jnp.sum(up_point * norm_point, axis=(0, 1)),
            jnp.sum(up_atrous, axis=(0, 1)),
            jnp.sum(up_atrous * norm_atrous, axis=(0, 1)),
        ]
    )
    branch_means = one_axis_at_a_time(local_sums, STRIP_SAMPLE) / position_count
    grad_point_b = ((up_point - branch_means[0] - norm_point * branch_means[1]) * scales[0]).astype(
        jnp.bfloat16
    )
    grad_atrous_b = (
        (up_atrous - branch_means[2] - norm_atrous * branch_means[3]) * scales[1]
    ).astype(jnp.bfloat16)
    input_grad = contract_last(grad_point_b, point_full) + grad_pool / map_area
    column_sets = []
    for row_stride in (-1, 0, 1):
        if row_stride == 0:
            source = grad_atrous_b
        else:
            source = passed_along(grad_atrous_b, STRIP, row_stride * strip_extent)
        stacked = column_stack(source)
        column_sets.append(stacked)
        input_grad = input_grad + contract_last(stacked, tap_rows(row_stride))
    image_gate = jnp.where(lax.axis_index(STRIP) == 0, 1.0, 0.0).astype(jnp.float32)
    columns_all = jnp.concatenate([grad_point_b] + column_sets, -1).reshape(
        strip_row_count * col_count, 10 * out_width
    )
    flat_map = sample_map.reshape(strip_row_count * col_count, chan_count)
    image_cols = grad_image_b.astype(jnp.float32) * (image_gate * factor)
    pooled_wide = pooled.astype(jnp.float32)
    proj_local = (
        lax.dot_general(
            relu_joined.reshape(-1, 2 * out_width),
            grad_mix_b.reshape(-1, out_width),
            (((0,), (0,)), ((), ())),
            preferred_element_type=jnp.float32,
        )
        * factor
    )
    proj_image = (
        relu_image.astype(jnp.float32)[:, None]
        * (column_b.astype(jnp.float32) * (image_gate * factor))[None, :]
    )
    proj_shard = sum_at_owner(
        jnp.concatenate([proj_local, proj_image], 0).astype(jnp.bfloat16), SAMPLE, 0
    )
    chan_piece = chan_count // (samples * strips)
    swapped_map = (
        flat_map.reshape(strip_row_count * col_count, samples, strips, chan_piece)
        .transpose(0, 2, 1, 3)
        .reshape(strip_row_count * col_count, chan_count)
    )
    swapped_pool = (
        pooled_wide.reshape(samples, strips, chan_piece).transpose(1, 0, 2).reshape(chan_count)
    )
    tap_terms = (
        lax.dot_general(
            swapped_map, columns_all, (((0,), (0,)), ((), ())), preferred_element_type=jnp.float32
        )
        * factor
    )
    strip_section = lax.psum_scatter(
        jnp.concatenate([tap_terms, swapped_pool[:, None] * image_cols[None, :]], 1).astype(
            jnp.bfloat16
        ),
        STRIP,
        scatter_dimension=0,
        tiled=True,
    )
    shard_part = sum_at_owner(strip_section, SAMPLE, 0)
    weight_total = gather_directly(shard_part.astype(jnp.bfloat16), STRIP, 0).astype(
        shard_part.dtype
    )
    proj_total = total_of_pieces(proj_shard.astype(jnp.bfloat16), STRIP).astype(jnp.float32)
    return (
        result[None],
        input_grad.astype(jnp.bfloat16)[None],
        weight_total[:, :out_width],
        weight_total[:, out_width : 10 * out_width],
        weight_total[:, 10 * out_width :],
        proj_total,
    )


def solution(mesh):
    finer = Mesh(mesh.devices.reshape(8, 2, 4, 4), ("strip_0", "strip_1", "sample_0", "sample_1"))
    placed = (
        P(SAMPLE, STRIP, None, None),
        P(SAMPLE, None),
        P(SAMPLE, None),
        P(SAMPLE, None),
        P(SAMPLE, None),
        P(SAMPLE, STRIP, None, None),
    )
    return jax.shard_map(
        on_device,
        mesh=finer,
        in_specs=placed,
        out_specs=(
            P(SAMPLE, STRIP, None, None),
            P(SAMPLE, STRIP, None, None),
            P(SAMPLE, None),
            P(SAMPLE, None),
            P(SAMPLE, None),
            P(SAMPLE, None),
        ),
        check_vma=False,
    )
```

profile of v0, /device:TPU:1, one launch (start us, length us, event | category | flops | bytes accessed | tf_op | source)
XLA Modules:
  0.0 485.7 jit_solution(9308870175237719834)
XLA Ops:
  10.3 10.0 %all-to-all-start = ((f32[16,1,2048]{2,1,0:T(1,128)}), f32[16,1,2048]{2,1,0:T(1,128)}, u32[]{:S(2)}, u32[]{:S(2)}) async-start(f32[16,1,2048]{2,1,0:T(1,128)} %broadcast_in_dim.10), calls=%async_computation | async-start | bytes 262144 | tf_op jit(solution)/shard_map/all_to_all | solution.py:31
  20.3 5.3 %collective-permute-start.1 = (bf16[3,108,2048]{2,1,0:T(8,128)(2,1)S(1)}, bf16[3,108,2048]{2,1,0:T(8,128)(2,1)}, u32[]{:S(2)}, u32[]{:S(2)}) collective-permute-start(bf16[3,108,2048]{2,1,0:T(8,128)(2,1)S(1)} %bitcast.155), channel_id=1, source_target_pairs={{0,64},{16,80},{32,96},{48,112},{64,128},{80,144},{96,160},{112,17... | collective-permute-start | bytes 3981320 | tf_op jit(solution)/shard_map/ppermute | solution.py:43
  33.8 20.7 %all_gather.13 = bf16[768,256]{1,0:T(8,128)(2,1)S(1)} all-gather(bf16[48,256]{1,0:T(8,128)(2,1)S(1)} %copy-done.17), channel_id=1, replica_groups=mesh['strip_0'=8,'strip_1'=2,'sample_0'=4,'sample_1'=4] {'sample_0','sam..., dimensions={0}, use_global_device_ids=true | all-gather | bytes 417792 | tf_op jit(solution)/shard_map/all_gather | solution.py:146
  55.9 49.2 %all-gather.3.cloned.1.call-done = bf16[2048,2816]{1,0:T(8,128)(2,1)} async-done(((bf16[128,2816]{1,0:T(8,128)(2,1)}), bf16[2048,2816]{1,0:T(8,128)(2,1)}) %all-gather.3.cloned.1.call-update) | async-done | bytes 11534352 | tf_op jit(solution)/shard_map/all_gather | solution.py:25
  120.7 14.3 %all-reduce.11 = (f32[2,256]{1,0:T(2,128)S(1)}, f32[2,256]{1,0:T(2,128)S(1)}) all-reduce(f32[2,256]{1,0:T(2,128)S(1)} %get-tuple-element.88, f32[2,256]{1,0:T(2,128)S(1)} %get-tuple-element.87), channel_id=1, replica_groups=mesh['strip_0'=8,'strip_1'=2,'sample_0'=4,'sample_1'=4] {'strip_0'}, use_global_device_ids=true, to_apply=%region_8.9 | all-reduce | flops 1024 | bytes 8192 | tf_op jit(solution)/shard_map/psum | solution.py:18
  135.0 6.3 %all-reduce.20 = (f32[2,256]{1,0:T(2,128)S(1)}, f32[2,256]{1,0:T(2,128)S(1)}) all-reduce(f32[2,256]{1,0:T(2,128)S(1)} %get-tuple-element.26, f32[2,256]{1,0:T(2,128)S(1)} %get-tuple-element.27), channel_id=1, replica_groups=mesh['strip_0'=8,'strip_1'=2,'sample_0'=4,'sample_1'=4] {'strip_1'}, use_global_device_ids=true, to_apply=%region_9.10 | all-reduce | flops 1024 | bytes 8192 | tf_op jit(solution)/shard_map/psum | solution.py:18
  141.3 8.1 %all-reduce.17 = (f32[2,256]{1,0:T(2,128)S(1)}, f32[2,256]{1,0:T(2,128)S(1)}) all-reduce(f32[2,256]{1,0:T(2,128)S(1)} %get-tuple-element.44, f32[2,256]{1,0:T(2,128)S(1)} %get-tuple-element.45), channel_id=1, replica_groups=mesh['strip_0'=8,'strip_1'=2,'sample_0'=4,'sample_1'=4] {'sample_0'}, use_global_device_ids=true, to_apply=%region_10.11 | all-reduce | flops 1024 | bytes 8192 | tf_op jit(solution)/shard_map/psum | solution.py:18
  149.4 6.5 %all-reduce.14 = (f32[2,256]{1,0:T(2,128)S(1)}, f32[2,256]{1,0:T(2,128)S(1)}) all-reduce(f32[2,256]{1,0:T(2,128)S(1)} %get-tuple-element.38, f32[2,256]{1,0:T(2,128)S(1)} %get-tuple-element.39), channel_id=1, replica_groups=mesh['strip_0'=8,'strip_1'=2,'sample_0'=4,'sample_1'=4] {'sample_1'}, use_global_device_ids=true, to_apply=%region_11.12 | all-reduce | flops 1024 | bytes 8192 | tf_op jit(solution)/shard_map/psum | solution.py:18
  156.6 11.5 %all-reduce.10 = (f32[1,256]{1,0:T(1,128)S(1)}, f32[1,256]{1,0:T(1,128)S(1)}) all-reduce(f32[1,256]{1,0:T(1,128)S(1)} %bitcast.198, f32[1,256]{1,0:T(1,128)S(1)} %bitcast.197), channel_id=1, replica_groups=mesh['strip_0'=8,'strip_1'=2,'sample_0'=4,'sample_1'=4] {'strip_0'}, use_global_device_ids=true, to_apply=%region_22.23 | all-reduce | flops 512 | bytes 4096 | tf_op jit(solution)/shard_map/psum | solution.py:18
  168.2 10.2 %all-reduce.19 = (f32[1,256]{1,0:T(1,128)S(1)}, f32[1,256]{1,0:T(1,128)S(1)}) all-reduce(f32[1,256]{1,0:T(1,128)S(1)} %get-tuple-element.24, f32[1,256]{1,0:T(1,128)S(1)} %get-tuple-element.25), channel_id=1, replica_groups=mesh['strip_0'=8,'strip_1'=2,'sample_0'=4,'sample_1'=4] {'strip_1'}, use_global_device_ids=true, to_apply=%region_23.24 | all-reduce | flops 512 | bytes 4096 | tf_op jit(solution)/shard_map/psum | solution.py:18
  178.4 6.8 %all-reduce.16 = (f32[1,256]{1,0:T(1,128)S(1)}, f32[1,256]{1,0:T(1,128)S(1)}) all-reduce(f32[1,256]{1,0:T(1,128)S(1)} %get-tuple-element.42, f32[1,256]{1,0:T(1,128)S(1)} %get-tuple-element.43), channel_id=1, replica_groups=mesh['strip_0'=8,'strip_1'=2,'sample_0'=4,'sample_1'=4] {'sample_0'}, use_global_device_ids=true, to_apply=%region_24.25 | all-reduce | flops 512 | bytes 4096 | tf_op jit(solution)/shard_map/psum | solution.py:18
  185.2 6.1 %all-reduce.13 = (f32[1,256]{1,0:T(1,128)S(1)}, f32[1,256]{1,0:T(1,128)S(1)}) all-reduce(f32[1,256]{1,0:T(1,128)S(1)} %get-tuple-element.36, f32[1,256]{1,0:T(1,128)S(1)} %get-tuple-element.37), channel_id=1, replica_groups=mesh['strip_0'=8,'strip_1'=2,'sample_0'=4,'sample_1'=4] {'sample_1'}, use_global_device_ids=true, to_apply=%region_25.26 | all-reduce | flops 512 | bytes 4096 | tf_op jit(solution)/shard_map/psum | solution.py:18
  191.6 11.4 %all-reduce.9 = (f32[256]{0:T(256)S(1)}, f32[256]{0:T(256)S(1)}) all-reduce(f32[256]{0:T(256)S(1)} %get-tuple-element.13, f32[256]{0:T(256)S(1)} %get-tuple-element.12), channel_id=1, replica_groups=mesh['strip_0'=8,'strip_1'=2,'sample_0'=4,'sample_1'=4] {'strip_0'}, use_global_device_ids=true, to_apply=%region_32.33 | all-reduce | flops 512 | bytes 4096 | tf_op jit(solution)/shard_map/psum | solution.py:18
  202.9 9.8 %all-reduce.18 = (f32[256]{0:T(256)S(1)}, f32[256]{0:T(256)S(1)}) all-reduce(f32[256]{0:T(256)S(1)} %get-tuple-element.22, f32[256]{0:T(256)S(1)} %get-tuple-element.23), channel_id=1, replica_groups=mesh['strip_0'=8,'strip_1'=2,'sample_0'=4,'sample_1'=4] {'strip_1'}, use_global_device_ids=true, to_apply=%region_33.34 | all-reduce | flops 512 | bytes 4096 | tf_op jit(solution)/shard_map/psum | solution.py:18
  212.7 7.7 %all-reduce.15 = (f32[256]{0:T(256)S(1)}, f32[256]{0:T(256)S(1)}) all-reduce(f32[256]{0:T(256)S(1)} %get-tuple-element.40, f32[256]{0:T(256)S(1)} %get-tuple-element.41), channel_id=1, replica_groups=mesh['strip_0'=8,'strip_1'=2,'sample_0'=4,'sample_1'=4] {'sample_0'}, use_global_device_ids=true, to_apply=%region_34.35 | all-reduce | flops 512 | bytes 4096 | tf_op jit(solution)/shard_map/psum | solution.py:18
  220.4 6.5 %all-reduce.12 = (f32[256]{0:T(256)S(1)}, f32[256]{0:T(256)S(1)}) all-reduce(f32[256]{0:T(256)S(1)} %get-tuple-element.34, f32[256]{0:T(256)S(1)} %get-tuple-element.35), channel_id=1, replica_groups=mesh['strip_0'=8,'strip_1'=2,'sample_0'=4,'sample_1'=4] {'sample_1'}, use_global_device_ids=true, to_apply=%region_35.36 | all-reduce | flops 512 | bytes 4096 | tf_op jit(solution)/shard_map/psum | solution.py:18
  228.5 11.5 %psum.220 = f32[4,256]{1,0:T(4,128)S(1)} all-reduce(f32[4,256]{1,0:T(4,128)S(1)} %pad_maximum_fusion.6), channel_id=1, replica_groups=mesh['strip_0'=8,'strip_1'=2,'sample_0'=4,'sample_1'=4] {'strip_0'}, use_global_device_ids=true, to_apply=%region_40.41 | all-reduce | flops 1024 | bytes 8192 | tf_op jit(solution)/shard_map/psum | solution.py:18
  240.0 10.3 %psum.221 = f32[4,256]{1,0:T(4,128)S(1)} all-reduce(f32[4,256]{1,0:T(4,128)S(1)} %psum.220), channel_id=1, replica_groups=mesh['strip_0'=8,'strip_1'=2,'sample_0'=4,'sample_1'=4] {'strip_1'}, use_global_device_ids=true, to_apply=%region_41.42 | all-reduce | flops 1024 | bytes 8192 | tf_op jit(solution)/shard_map/psum | solution.py:18
  250.3 6.8 %psum.222 = f32[4,256]{1,0:T(4,128)S(1)} all-reduce(f32[4,256]{1,0:T(4,128)S(1)} %psum.221), channel_id=1, replica_groups=mesh['strip_0'=8,'strip_1'=2,'sample_0'=4,'sample_1'=4] {'sample_0'}, use_global_device_ids=true, to_apply=%region_42.43 | all-reduce | flops 1024 | bytes 8192 | tf_op jit(solution)/shard_map/psum | solution.py:18
  257.1 6.1 %psum.223 = f32[4,256]{1,0:T(4,128)S(1)} all-reduce(f32[4,256]{1,0:T(4,128)S(1)} %psum.222), channel_id=1, replica_groups=mesh['strip_0'=8,'strip_1'=2,'sample_0'=4,'sample_1'=4] {'sample_1'}, use_global_device_ids=true, to_apply=%region_43.44 | all-reduce | flops 1024 | bytes 8192 | tf_op jit(solution)/shard_map/psum | solution.py:18
  267.3 13.6 %all-to-all-start.1 = ((f32[16,1,256]{2,1,0:T(1,128)}), f32[16,1,256]{2,1,0:T(1,128)S(1)}, u32[]{:S(2)}, u32[]{:S(2)}) async-start(f32[16,1,256]{2,1,0:T(1,128)} %broadcast_in_dim.12), calls=%async_computation.1 | async-start | bytes 32768 | tf_op jit(solution)/shard_map/all_to_all | solution.py:31
  282.1 6.2 %all-to-all-done.1 = f32[16,1,256]{2,1,0:T(1,128)S(1)} async-done(((f32[16,1,256]{2,1,0:T(1,128)}), f32[16,1,256]{2,1,0:T(1,128)S(1)}, u32[]{:S(2)}, u32[]{:S(2)}) %all-to-all-start.1) | async-done | bytes 16416 | tf_op jit(solution)/shard_map/all_to_all | solution.py:31
  301.1 7.6 %fusion = bf16[2048,2560]{0,1:T(8,128)(2,1)S(1)} fusion(bf16[324,2560]{1,0:T(8,128)(2,1)} %reshape.81, bf16[324,2048]{0,1:T(8,128)(2,1)} %bitcast.157), kind=kOutput, calls=%fused_computation.2 | convolution fusion | flops 3407872000 | bytes 13471744 | tf_op jit(solution)/shard_map/dot_general | solution.py:260
  308.8 11.3 %pad_maximum_fusion = bf16[2048,2816]{0,1:T(8,128)(2,1)} fusion(bf16[2048,256]{0,1:T(8,128)(2,1)S(1)} %multiply_convert_fusion.1, bf16[2048,2560]{0,1:T(8,128)(2,1)S(1)} %fusion), kind=kLoop, calls=%fused_computation.1 | loop fusion | flops 23068672 | bytes 23068672 | tf_op jit(solution)/shard_map/concatenate | solution.py:266
  320.1 15.3 %copy.30 = bf16[2048,2816]{1,0:T(8,128)(2,1)} copy(bf16[2048,2816]{0,1:T(8,128)(2,1)} %pad_maximum_fusion) | data formatting | bytes 23068672
  335.7 67.2 %reduce-scatter.4.cloned.1.call-done = bf16[128,2816]{1,0:T(8,128)(2,1)} async-done(((bf16[2048,2816]{1,0:T(8,128)(2,1)}), bf16[128,2816]{1,0:T(8,128)(2,1)}) %reduce-scatter.4.cloned.1.call-update) | async-done | bytes 720912 | tf_op jit(solution)/shard_map/reduce_scatter | solution.py:265
  403.0 6.4 %all-to-all-start.2 = ((bf16[16,8,2816]{2,1,0:T(8,128)(2,1)}), bf16[16,8,2816]{2,1,0:T(8,128)(2,1)S(1)}, u32[]{:S(2)}, u32[]{:S(2)}) async-start(bf16[16,8,2816]{2,1,0:T(8,128)(2,1)} %bitcast.159), calls=%async_computation.2 | async-start | bytes 1441792 | tf_op jit(solution)/shard_map/all_to_all | solution.py:53
  411.9 7.8 %all-to-all-done.2 = bf16[16,8,2816]{2,1,0:T(8,128)(2,1)S(1)} async-done(((bf16[16,8,2816]{2,1,0:T(8,128)(2,1)}), bf16[16,8,2816]{2,1,0:T(8,128)(2,1)S(1)}, u32[]{:S(2)}, u32[]{:S(2)}) %all-to-all-start.2) | async-done | bytes 720928 | tf_op jit(solution)/shard_map/all_to_all | solution.py:53
  427.2 4.9 %all-to-all-done.4 = bf16[16,48,256]{2,1,0:T(8,128)(2,1)} async-done(((bf16[16,48,256]{2,1,0:T(8,128)(2,1)}), bf16[16,48,256]{2,1,0:T(8,128)(2,1)}, u32[]{:S(2)}, u32[]{:S(2)}) %all-to-all-start.4) | async-done | bytes 393248 | tf_op jit(solution)/shard_map/all_to_all | solution.py:53
  433.1 11.1 %all-to-all-start.3 = ((bf16[16,8,2816]{2,1,0:T(8,128)(2,1)}), bf16[16,8,2816]{2,1,0:T(8,128)(2,1)}, u32[]{:S(2)}, u32[]{:S(2)}) async-start(bf16[16,8,2816]{2,1,0:T(8,128)(2,1)} %broadcast_in_dim.14), calls=%async_computation.3 | async-start | bytes 1441792 | tf_op jit(solution)/shard_map/all_to_all | solution.py:31
  450.8 4.3 fusion.2
  456.2 19.0 %all-gather = bf16[768,256]{1,0:T(8,128)(2,1)S(1)} all-gather(bf16[48,256]{1,0:T(8,128)(2,1)S(1)} %reduce_sum.234), channel_id=2, replica_groups=mesh['strip_0'=8,'strip_1'=2,'sample_0'=4,'sample_1'=4] {'strip_0','stri..., dimensions={0}, use_global_device_ids=true | all-gather | bytes 417792 | tf_op jit(solution)/shard_map/all_gather | solution.py:69
  (129 shorter events, 68.3 us)
Async XLA Ops:
  7.2 2.2 copy-start.1
  7.2 97.9 %all-gather.3.cloned.1.call-start = ((), (), s32[]{:S(2)}) async-start(), calls=%async_computation.6 | async-start | bytes 12255232 | tf_op jit(solution)/shard_map/all_gather | solution.py:25
  10.3 44.2 %all-to-all-start = ((f32[16,1,2048]{2,1,0:T(1,128)}), f32[16,1,2048]{2,1,0:T(1,128)}, u32[]{:S(2)}, u32[]{:S(2)}) async-start(f32[16,1,2048]{2,1,0:T(1,128)} %broadcast_in_dim.10), calls=%async_computation | async-start | bytes 262144 | tf_op jit(solution)/shard_map/all_to_all | solution.py:31
  20.3 92.2 %collective-permute-start.1 = (bf16[3,108,2048]{2,1,0:T(8,128)(2,1)S(1)}, bf16[3,108,2048]{2,1,0:T(8,128)(2,1)}, u32[]{:S(2)}, u32[]{:S(2)}) collective-permute-start(bf16[3,108,2048]{2,1,0:T(8,128)(2,1)S(1)} %bitcast.155), channel_id=1, source_target_pairs={{0,64},{16,80},{32,96},{48,112},{64,128},{80,144},{96,160},{112,17... | collective-permute-start | bytes 3981320 | tf_op jit(solution)/shard_map/ppermute | solution.py:43
  25.6 91.5 %collective-permute-start = (bf16[3,108,2048]{2,1,0:T(8,128)(2,1)S(1)}, bf16[3,108,2048]{2,1,0:T(8,128)(2,1)}, u32[]{:S(2)}, u32[]{:S(2)}) collective-permute-start(bf16[3,108,2048]{2,1,0:T(8,128)(2,1)S(1)} %bitcast.156), channel_id=1, source_target_pairs={{64,0},{80,16},{96,32},{112,48},{128,64},{144,80},{160,96},{176,11... | collective-permute-start | bytes 3981320 | tf_op jit(solution)/shard_map/ppermute | solution.py:43
  31.0 2.8 copy-start.17
  54.5 173.4 %copy-start.10 = (bf16[768,256]{1,0:T(8,128)(2,1)}, bf16[768,256]{1,0:T(8,128)(2,1)S(1)}, u32[]{:S(2)}) copy-start(bf16[768,256]{1,0:T(8,128)(2,1)S(1)} %all_gather.13) | copy-start | bytes 1179652
  109.2 5.2 %copy-start = (bf16[2048,2816]{1,0:T(8,128)(2,1)S(1)}, bf16[2048,2816]{1,0:T(8,128)(2,1)}, u32[]{:S(2)}) copy-start(bf16[2048,2816]{1,0:T(8,128)(2,1)} %all-gather.3.cloned.1.call-done) | copy-start | bytes 34603012
  120.6 170.7 %copy-start.2 = (f32[256,3,108]{0,2,1:T(8,128)}, f32[256,3,108]{0,2,1:T(8,128)S(1)}, u32[]{:S(2)}) copy-start(f32[256,3,108]{0,2,1:T(8,128)S(1)} %get-tuple-element.85) | copy-start | bytes 995332
  120.6 70.7 %copy-start.13 = (bf16[1,3,108,256]{3,2,1,0:T(8,128)(2,1)S(1)}, bf16[1,3,108,256]{3,2,1,0:T(8,128)(2,1)}, u32[]{:S(2)}) copy-start(bf16[1,3,108,256]{3,2,1,0:T(8,128)(2,1)} %param.11) | copy-start | bytes 497668
  263.5 31.8 %copy-start.6 = (bf16[3,108,256]{2,1,0:T(8,128)(2,1)}, bf16[3,108,256]{2,1,0:T(8,128)(2,1)S(1)}, u32[]{:S(2)}) copy-start(bf16[3,108,256]{2,1,0:T(8,128)(2,1)S(1)} %multiply_convert_fusion.2) | copy-start | bytes 497668
  263.5 32.7 %collective-permute-start.3 = (bf16[3,108,256]{2,1,0:T(8,128)(2,1)S(1)}, bf16[3,108,256]{2,1,0:T(8,128)(2,1)S(1)}, u32[]{:S(2)}, u32[]{:S(2)}) collective-permute-start(bf16[3,108,256]{2,1,0:T(8,128)(2,1)S(1)} %multiply_convert_fusion.2), channel_id=1, source_target_pairs={{0,64},{16,80},{32,96},{48,112},{64,128},{80,144},{96,160},{112,17... | collective-permute-start | bytes 497672 | tf_op jit(solution)/shard_map/ppermute | solution.py:43
  265.4 26.2 %collective-permute-start.2 = (bf16[3,108,256]{2,1,0:T(8,128)(2,1)S(1)}, bf16[3,108,256]{2,1,0:T(8,128)(2,1)S(1)}, u32[]{:S(2)}, u32[]{:S(2)}) collective-permute-start(bf16[3,108,256]{2,1,0:T(8,128)(2,1)S(1)} %multiply_convert_fusion.2), channel_id=1, source_target_pairs={{64,0},{80,16},{96,32},{112,48},{128,64},{144,80},{160,96},{176,11... | collective-permute-start | bytes 497672 | tf_op jit(solution)/shard_map/ppermute | solution.py:43
  267.3 21.0 %all-to-all-start.1 = ((f32[16,1,256]{2,1,0:T(1,128)}), f32[16,1,256]{2,1,0:T(1,128)S(1)}, u32[]{:S(2)}, u32[]{:S(2)}) async-start(f32[16,1,256]{2,1,0:T(1,128)} %broadcast_in_dim.12), calls=%async_computation.1 | async-start | bytes 32768 | tf_op jit(solution)/shard_map/all_to_all | solution.py:31
  280.9 122.0 %reduce-scatter.4.cloned.1.call-start = ((), (), s32[]{:S(2)}) async-start(), calls=%async_computation.7 | async-start | bytes 12255232 | tf_op jit(solution)/shard_map/reduce_scatter | solution.py:265
  291.5 9.6 %copy-start.4 = (bf16[3,108,256]{2,1,0:T(8,128)(2,1)}, bf16[3,108,256]{2,1,0:T(8,128)(2,1)S(1)}, u32[]{:S(2)}) copy-start(bf16[3,108,256]{2,1,0:T(8,128)(2,1)S(1)} %collective-permute-done.2) | copy-start | bytes 497668
  296.1 5.0 %copy-start.8 = (bf16[3,108,256]{2,1,0:T(8,128)(2,1)}, bf16[3,108,256]{2,1,0:T(8,128)(2,1)S(1)}, u32[]{:S(2)}) copy-start(bf16[3,108,256]{2,1,0:T(8,128)(2,1)S(1)} %collective-permute-done.3) | copy-start | bytes 497668
  403.0 16.8 %all-to-all-start.2 = ((bf16[16,8,2816]{2,1,0:T(8,128)(2,1)}), bf16[16,8,2816]{2,1,0:T(8,128)(2,1)S(1)}, u32[]{:S(2)}, u32[]{:S(2)}) async-start(bf16[16,8,2816]{2,1,0:T(8,128)(2,1)} %bitcast.159), calls=%async_computation.2 | async-start | bytes 1441792 | tf_op jit(solution)/shard_map/all_to_all | solution.py:53
  419.7 4.2 copy-start.3
  419.7 12.5 %all-to-all-start.4 = ((bf16[16,48,256]{2,1,0:T(8,128)(2,1)}), bf16[16,48,256]{2,1,0:T(8,128)(2,1)}, u32[]{:S(2)}, u32[]{:S(2)}) async-start(bf16[16,48,256]{2,1,0:T(8,128)(2,1)} %bitcast.45), calls=%async_computation.4 | async-start | bytes 786432 | tf_op jit(solution)/shard_map/all_to_all | solution.py:53
  426.0 18.2 %copy-start.7 = (bf16[3,108,256]{2,1,0:T(8,128)(2,1)S(1)}, bf16[3,108,256]{2,1,0:T(8,128)(2,1)}, u32[]{:S(2)}) copy-start(bf16[3,108,256]{2,1,0:T(8,128)(2,1)} %copy-done.6) | copy-start | bytes 497668
  426.0 18.2 %copy-start.16 = (bf16[3,108,256]{2,1,0:T(8,128)(2,1)S(1)}, bf16[3,108,256]{2,1,0:T(8,128)(2,1)}, u32[]{:S(2)}) copy-start(bf16[3,108,256]{2,1,0:T(8,128)(2,1)} %get-tuple-element.68) | copy-start | bytes 497668
  433.1 42.8 %all-to-all-start.3 = ((bf16[16,8,2816]{2,1,0:T(8,128)(2,1)}), bf16[16,8,2816]{2,1,0:T(8,128)(2,1)}, u32[]{:S(2)}, u32[]{:S(2)}) async-start(bf16[16,8,2816]{2,1,0:T(8,128)(2,1)} %broadcast_in_dim.14), calls=%async_computation.3 | async-start | bytes 1441792 | tf_op jit(solution)/shard_map/all_to_all | solution.py:31
  444.2 3.3 copy-start.5
  444.2 3.3 copy-start.11
  444.2 3.3 copy-start.12
  447.5 3.3 copy-start.9
  447.6 3.3 copy-start.14
  447.6 3.3 copy-start.15
Sparse Core Ops, SparseCore 0:
  11.0 94.0 all-gather.2
  335.5 67.3 reduce-scatter.3
where the time goes:
time: 487 us; the launch traced here: 486 us
  blocking collectives  180 us (37%)
  waiting for transfers between devices  135 us (28%)
  starting transfers between devices  55.3 us (11%)
  local copies, waits for them, and re-layouts  38.2 us (8%)
  matrix products  34.6 us (7%)
  other arithmetic  25.1 us (5%)
  between operations  17.3 us (4%)
    psum x16, blocking collectives, one_axis_at_a_time(): array = lax.psum(array, axis)  140 us
    reduce_scatter x1, waiting for transfers between devices, on_device(): lax.psum_scatter(jnp.concatenate([tap_terms, swapped_pool[:, None] * imag...  67.2 us
    all_gather x1, waiting for transfers between devices, side_by_side(): filled = lax.all_gather(both, axis, axis=dim, tiled=True)  49.2 us
    all_to_all x3, starting transfers between devices, from_everyone(): lax.all_to_all(jnp.broadcast_to(array[None], (peers, *array.shape)), axis...  34.7 us
    unnamed x46, local copies, waits for them, and re-layouts  24.8 us
    all_gather x1, blocking collectives, on_device(): lax.all_gather(w_proj, SAMPLE, axis=0, tiled=True)  20.7 us
    all_gather x1, blocking collectives, total_of_pieces(): return lax.all_gather(array, axis).astype(jnp.float32).sum(0)  19 us
    dot_general x7, matrix products, contract_last(): lax.dot_general(left, right, (((left.ndim - 1,), (1,)), ((), ())), prefer...  15.7 us
  transfers between devices with their start and end apart: 11, of which 5 were waited for; matrix products, arithmetic and copies ran while one was open for 9% of the time, Pallas kernels for 0%

commit v1 on v0

--- a/solution.py
+++ b/solution.py
@@ -1,6 +1,8 @@
 import jax
 import jax.numpy as jnp
 from jax import lax
+from jax.experimental import pallas as pl
+from jax.experimental.pallas import tpu as pltpu
 from jax.sharding import Mesh
 from jax.sharding import PartitionSpec as P
 
@@ -13,10 +15,71 @@
 EPSILON = 1e-05
 
 
-def one_axis_at_a_time(array, axes):
-    for axis in axes:
-        array = lax.psum(array, axis)
-    return array
+MESH_ID = pl.DeviceIdType.MESH
+
+
+def total_kernel(x_ref, strip_ref, out_ref, slots_a, slots_b, send_a, recv_a, send_b, recv_b):
+    strip = lax.axis_index("strip_0") * 2 + lax.axis_index("strip_1")
+    sample = lax.axis_index("sample_0") * 4 + lax.axis_index("sample_1")
+
+    def strip_peer(k):
+        other = lax.rem(strip + k, 16)
+        return {"strip_0": lax.div(other, 2), "strip_1": lax.rem(other, 2)}
+
+    def sample_peer(k):
+        other = lax.rem(sample + k, 16)
+        return {"sample_0": lax.div(other, 4), "sample_1": lax.rem(other, 4)}
+
+    barrier = pltpu.get_barrier_semaphore()
+    for k in range(1, 16):
+        pl.semaphore_signal(barrier, inc=1, device_id=strip_peer(k), device_id_type=MESH_ID)
+        pl.semaphore_signal(barrier, inc=1, device_id=sample_peer(k), device_id_type=MESH_ID)
+    pl.semaphore_wait(barrier, 30)
+
+    def stage(source, slots, me, peer, send, recv):
+        copies = []
+        for k in range(1, 16):
+            copy = pltpu.make_async_remote_copy(
+                src_ref=source,
+                dst_ref=slots.at[me],
+                send_sem=send.at[k - 1],
+                recv_sem=recv.at[k - 1],
+                device_id=peer(k),
+                device_id_type=MESH_ID,
+            )
+            copy.start()
+            copies.append(copy)
+        slots[me] = source[...]
+        for copy in copies:
+            copy.wait()
+        return jnp.sum(slots[...], axis=0)
+
+    strip_ref[...] = stage(x_ref, slots_a, strip, strip_peer, send_a, recv_a)
+    out_ref[...] = stage(strip_ref, slots_b, sample, sample_peer, send_b, recv_b)
+
+
+def mesh_total(array, call_id):
+    shape = array.shape
+    flat = array.reshape(-1, shape[-1])
+    rows, width = flat.shape
+    spec = pl.BlockSpec(memory_space=pltpu.VMEM)
+    strip_sum, total = pl.pallas_call(
+        total_kernel,
+        out_shape=[jax.ShapeDtypeStruct((rows, width), jnp.float32)] * 2,
+        in_specs=[spec],
+        out_specs=[spec, spec],
+        scratch_shapes=[
+            pltpu.VMEM((16, rows, width), jnp.float32),
+            pltpu.VMEM((16, rows, width), jnp.float32),
+            pltpu.SemaphoreType.DMA((15,)),
+            pltpu.SemaphoreType.DMA((15,)),
+            pltpu.SemaphoreType.DMA((15,)),
+            pltpu.SemaphoreType.DMA((15,)),
+        ],
+        compiler_params=pltpu.CompilerParams(collective_id=call_id, has_side_effects=True),
+        name=f"mesh_total_{call_id}",
+    )(flat)
+    return total.reshape(shape)
 
 
 def side_by_side(arrays, axis, dim, along):
@@ -118,13 +181,10 @@
     )
 
 
-def moments(values, position_count):
+def moments(values, position_count, call_id):
     branch_sums = jnp.stack([jnp.sum(tensor, axis=(0, 1)) for tensor in values])
     squares = jnp.stack([jnp.sum(jnp.square(tensor), axis=(0, 1)) for tensor in values])
-    totals, powers = (
-        one_axis_at_a_time(branch_sums, STRIP_SAMPLE),
-        one_axis_at_a_time(squares, STRIP_SAMPLE),
-    )
+    totals, powers = mesh_total(jnp.stack([branch_sums, squares]), call_id)
     centres = totals / position_count
     variances = powers / position_count - jnp.square(centres)
     return (centres, variances)
@@ -154,11 +214,12 @@
     point_out = jnp.dot(sample_map, point_full, preferred_element_type=jnp.float32)
     dilated_branch_output = row_part(sample_map, tap_rows(0), out_width)
     for row_stride in (1, -1):
-        remote = passed_along(sample_map, STRIP, -row_stride * strip_extent)
-        dilated_branch_output = dilated_branch_output + row_part(
-            remote, tap_rows(row_stride), out_width
+        dilated_branch_output = dilated_branch_output + passed_along(
+            row_part(sample_map, tap_rows(row_stride), out_width).astype(jnp.bfloat16),
+            STRIP,
+            -row_stride * strip_extent,
         )
-    centres, variances = moments([point_out, dilated_branch_output], position_count)
+    centres, variances = moments([point_out, dilated_branch_output], position_count, 0)
     scales = lax.rsqrt(variances + EPSILON)
     norm_point = (point_out - centres[0]) * scales[0]
     norm_atrous = (dilated_branch_output - centres[1]) * scales[1]
@@ -175,14 +236,13 @@
     mixed_out = mixed_out + jnp.dot(
         relu_image, proj_full[2 * out_width :], preferred_element_type=jnp.float32
     )
-    mix_centre, mix_spread = moments([mixed_out], position_count)
+    mix_centre, mix_spread = moments([mixed_out], position_count, 1)
     mix_scale = lax.rsqrt(mix_spread[0] + EPSILON)
     norm_mix = (mixed_out - mix_centre[0]) * mix_scale
     result = swish(norm_mix).astype(jnp.bfloat16)
     upstream = cotangent[0].astype(jnp.float32) * swish_slope(norm_mix)
-    first_sum, second_sum = (
-        one_axis_at_a_time(jnp.sum(upstream, axis=(0, 1)), STRIP_SAMPLE),
-        one_axis_at_a_time(jnp.sum(upstream * norm_mix, axis=(0, 1)), STRIP_SAMPLE),
+    first_sum, second_sum = mesh_total(
+        jnp.stack([jnp.sum(upstream, axis=(0, 1)), jnp.sum(upstream * norm_mix, axis=(0, 1))]), 2
     )
     grad_mix = (
         upstream - first_sum / position_count - norm_mix * (second_sum / position_count)
@@ -207,7 +267,7 @@
             jnp.sum(up_atrous * norm_atrous, axis=(0, 1)),
         ]
     )
-    branch_means = one_axis_at_a_time(local_sums, STRIP_SAMPLE) / position_count
+    branch_means = mesh_total(local_sums, 3) / position_count
     grad_point_b = ((up_point - branch_means[0] - norm_point * branch_means[1]) * scales[0]).astype(
         jnp.bfloat16
     )

time: 487 us -> 420 us (0.86)
  blocking collectives: 180 us -> 40.5 us
  Pallas kernels: 0 us -> 58.9 us
  waiting for transfers between devices: 135 us -> 153 us
    psum x16 -> x0, blocking collectives: 140 us -> none  [one_axis_at_a_time(): array = lax.psum(array, axis)]
    pallas_call x0 -> x4, Pallas kernels: none -> 58.9 us  [mesh_total(): pl.pallas_call(total_kernel, out_shape=[jax.ShapeDtypeStruct((rows, width...]
    ppermute x4, waiting for transfers between devices: 0.01 us -> 10.3 us  [passed_along(): return lax.ppermute(array, axis, pairs)]
    all_gather x1, waiting for transfers between devices: 49.2 us -> 55.6 us  [side_by_side(): filled = lax.all_gather(both, axis, axis=dim, tiled=True)]
    all_to_all x3, starting transfers between devices: 34.7 us -> 29.1 us  [from_everyone(): lax.all_to_all(jnp.broadcast_to(array[None], (peers, *array.shape)), axis...]
    unnamed x46 -> x44, local copies, waits for them, and re-layouts: 24.8 us -> 22.9 us
  transfers between devices with their start and end apart: 11 -> 11, of which waited for: 5 -> 6; matrix products, arithmetic and copies ran while one was open for 9% -> 9% of each run, Pallas kernels for 0% -> 0%
where the time goes in v1:
time: 420 us; the launch traced here: 419 us
  waiting for transfers between devices  153 us (36%)
  Pallas kernels  58.9 us (14%)
  starting transfers between devices  51.5 us (12%)
  blocking collectives  40.5 us (10%)
  local copies, waits for them, and re-layouts  36.9 us (9%)
  matrix products  31 us (7%)
  other arithmetic  29.7 us (7%)
  between operations  17.3 us (4%)
    reduce_scatter x1, waiting for transfers between devices, on_device(): lax.psum_scatter(jnp.concatenate([tap_terms, swapped_pool[:, None] * imag...  67.8 us
    pallas_call x4, Pallas kernels, mesh_total(): pl.pallas_call(total_kernel, out_shape=[jax.ShapeDtypeStruct((rows, width...  58.9 us
    all_gather x1, waiting for transfers between devices, side_by_side(): filled = lax.all_gather(both, axis, axis=dim, tiled=True)  55.6 us
    all_to_all x3, starting transfers between devices, from_everyone(): lax.all_to_all(jnp.broadcast_to(array[None], (peers, *array.shape)), axis...  29.1 us
    unnamed x44, local copies, waits for them, and re-layouts  22.9 us
    all_gather x1, blocking collectives, on_device(): lax.all_gather(w_proj, SAMPLE, axis=0, tiled=True)  21.5 us
    all_gather x1, blocking collectives, total_of_pieces(): return lax.all_gather(array, axis).astype(jnp.float32).sum(0)  19 us
    dot_general x7, matrix products, contract_last(): lax.dot_general(left, right, (((left.ndim - 1,), (1,)), ((), ())), prefer...  14.8 us
  transfers between devices with their start and end apart: 11, of which 6 were waited for; matrix products, arithmetic and copies ran while one was open for 9% of the time, Pallas kernels for 0%

profile of v1, /device:TPU:1, one launch (start us, length us, event | category | flops | bytes accessed | tf_op | source)
XLA Modules:
  0.0 418.7 jit_solution(16724395124989656089)
XLA Ops:
  7.2 2.1 pad_maximum_fusion.1
  10.3 10.0 %all-to-all-start = ((f32[16,1,2048]{2,1,0:T(1,128)}), f32[16,1,2048]{2,1,0:T(1,128)}, u32[]{:S(2)}, u32[]{:S(2)}) async-start(f32[16,1,2048]{2,1,0:T(1,128)} %broadcast_in_dim.10), calls=%async_computation | async-start | bytes 262144 | tf_op jit(solution)/shard_map/all_to_all | solution.py:94
  21.8 2.6 reshape_reshape_squeeze.3
  24.4 2.8 copy.27
  27.2 21.5 %all_gather.13 = bf16[768,256]{1,0:T(8,128)(2,1)S(1)} all-gather(bf16[48,256]{1,0:T(8,128)(2,1)S(1)} %copy-done.16), channel_id=1, replica_groups=mesh['strip_0'=8,'strip_1'=2,'sample_0'=4,'sample_1'=4] {'sample_0','sam..., dimensions={0}, use_global_device_ids=true | all-gather | bytes 417792 | tf_op jit(solution)/shard_map/all_gather | solution.py:206
  50.0 55.6 %all-gather.3.cloned.1.call-done = bf16[2048,2816]{1,0:T(8,128)(2,1)} async-done(((bf16[128,2816]{1,0:T(8,128)(2,1)}), bf16[2048,2816]{1,0:T(8,128)(2,1)}) %all-gather.3.cloned.1.call-update) | async-done | bytes 11534352 | tf_op jit(solution)/shard_map/all_gather | solution.py:88
  109.7 3.3 fusion.12
  113.2 4.4 %collective-permute-start.1 = (bf16[3,108,256]{2,1,0:T(8,128)(2,1)S(1)}, bf16[3,108,256]{2,1,0:T(8,128)(2,1)S(1)}, u32[]{:S(2)}, u32[]{:S(2)}) collective-permute-start(bf16[3,108,256]{2,1,0:T(8,128)(2,1)S(1)} %fusion.51), channel_id=1, source_target_pairs={{0,64},{16,80},{32,96},{48,112},{64,128},{80,144},{96,160},{112,17... | collective-permute-start | bytes 497672 | tf_op jit(solution)/shard_map/ppermute | solution.py:106
  122.6 10.3 %collective-permute-done = bf16[3,108,256]{2,1,0:T(8,128)(2,1)S(1)} collective-permute-done((bf16[3,108,256]{2,1,0:T(8,128)(2,1)S(1)}, bf16[3,108,256]{2,1,0:T(8,128)(2,1)S(1)}, u32[]{:S(2)}, u32[]{:S(2)}) %collective-permute-start) | collective-permute-done | bytes 165920 | tf_op jit(solution)/shard_map/ppermute | solution.py:106
  133.7 15.6 %mesh_total_0.1 = (f32[4,256]{1,0:T(4,128)}, f32[4,256]{1,0:T(4,128)}) custom-call(f32[4,256]{1,0:T(4,128)} %reshape.111.x_ref), custom_call_target="tpu_custom_call" | custom-call | tf_op jit(solution)/shard_map/mesh_total_0/pallas_call | solution.py:66
  151.1 14.3 %mesh_total_1.1 = (f32[2,256]{1,0:T(2,128)}, f32[2,256]{1,0:T(2,128)}) custom-call(f32[2,256]{1,0:T(2,128)} %maximum_bitcast_fusion.2.x_ref), custom_call_target="tpu_custom_call" | custom-call | tf_op jit(solution)/shard_map/mesh_total_1/pallas_call | solution.py:66
  167.0 14.4 %mesh_total_2.1 = (f32[2,256]{1,0:T(2,128)}, f32[2,256]{1,0:T(2,128)}) custom-call(f32[2,256]{1,0:T(2,128)} %pad_maximum_fusion.8.x_ref), custom_call_target="tpu_custom_call" | custom-call | tf_op jit(solution)/shard_map/mesh_total_2/pallas_call | solution.py:66
  184.3 14.7 %mesh_total_3.1 = (f32[4,256]{1,0:T(4,128)}, f32[4,256]{1,0:T(4,128)}) custom-call(f32[4,256]{1,0:T(4,128)} %pad_maximum_fusion.7.x_ref), custom_call_target="tpu_custom_call" | custom-call | tf_op jit(solution)/shard_map/mesh_total_3/pallas_call | solution.py:66
  199.8 4.2 collective-permute-start.3
  205.9 8.3 %all-to-all-start.1 = ((f32[16,1,256]{2,1,0:T(1,128)}), f32[16,1,256]{2,1,0:T(1,128)S(1)}, u32[]{:S(2)}, u32[]{:S(2)}) async-start(f32[16,1,256]{2,1,0:T(1,128)} %broadcast_in_dim.12), calls=%async_computation.1 | async-start | bytes 32768 | tf_op jit(solution)/shard_map/all_to_all | solution.py:94
  215.4 6.2 %all-to-all-done.1 = f32[16,1,256]{2,1,0:T(1,128)S(1)} async-done(((f32[16,1,256]{2,1,0:T(1,128)}), f32[16,1,256]{2,1,0:T(1,128)S(1)}, u32[]{:S(2)}, u32[]{:S(2)}) %all-to-all-start.1) | async-done | bytes 16416 | tf_op jit(solution)/shard_map/all_to_all | solution.py:94
  230.8 2.7 reshape.113
  233.5 7.6 %fusion = bf16[2048,2560]{0,1:T(8,128)(2,1)S(1)} fusion(bf16[324,2560]{1,0:T(8,128)(2,1)} %reshape.113, bf16[324,2048]{0,1:T(8,128)(2,1)} %bitcast.173), kind=kOutput, calls=%fused_computation.2 | convolution fusion | flops 3407872000 | bytes 13471744 | tf_op jit(solution)/shard_map/dot_general | solution.py:320
  241.1 11.3 %pad_maximum_fusion = bf16[2048,2816]{0,1:T(8,128)(2,1)} fusion(bf16[2048,256]{0,1:T(8,128)(2,1)S(1)} %multiply_convert_fusion.1, bf16[2048,2560]{0,1:T(8,128)(2,1)S(1)} %fusion), kind=kLoop, calls=%fused_computation.1 | loop fusion | flops 23068672 | bytes 23068672 | tf_op jit(solution)/shard_map/concatenate | solution.py:326
  252.5 15.3 %copy.30 = bf16[2048,2816]{1,0:T(8,128)(2,1)} copy(bf16[2048,2816]{0,1:T(8,128)(2,1)} %pad_maximum_fusion) | data formatting | bytes 23068672
  268.1 67.8 %reduce-scatter.4.cloned.1.call-done = bf16[128,2816]{1,0:T(8,128)(2,1)} async-done(((bf16[2048,2816]{1,0:T(8,128)(2,1)}), bf16[128,2816]{1,0:T(8,128)(2,1)}) %reduce-scatter.4.cloned.1.call-update) | async-done | bytes 720912 | tf_op jit(solution)/shard_map/reduce_scatter | solution.py:325
  335.9 6.5 %all-to-all-start.2 = ((bf16[16,8,2816]{2,1,0:T(8,128)(2,1)}), bf16[16,8,2816]{2,1,0:T(8,128)(2,1)S(1)}, u32[]{:S(2)}, u32[]{:S(2)}) async-start(bf16[16,8,2816]{2,1,0:T(8,128)(2,1)} %bitcast.175), calls=%async_computation.2 | async-start | bytes 1441792 | tf_op jit(solution)/shard_map/all_to_all | solution.py:116
  343.3 1.6 fusion.23
  344.9 8.0 %all-to-all-done.2 = bf16[16,8,2816]{2,1,0:T(8,128)(2,1)S(1)} async-done(((bf16[16,8,2816]{2,1,0:T(8,128)(2,1)}), bf16[16,8,2816]{2,1,0:T(8,128)(2,1)S(1)}, u32[]{:S(2)}, u32[]{:S(2)}) %all-to-all-start.2) | async-done | bytes 720928 | tf_op jit(solution)/shard_map/all_to_all | solution.py:116
  352.9 4.2 %all-to-all-start.4 = ((bf16[16,48,256]{2,1,0:T(8,128)(2,1)}), bf16[16,48,256]{2,1,0:T(8,128)(2,1)}, u32[]{:S(2)}, u32[]{:S(2)}) async-start(bf16[16,48,256]{2,1,0:T(8,128)(2,1)} %bitcast.52), calls=%async_computation.4 | async-start | bytes 786432 | tf_op jit(solution)/shard_map/all_to_all | solution.py:116
  357.1 2.0 convolution_add_fusion
  360.4 4.9 %all-to-all-done.4 = bf16[16,48,256]{2,1,0:T(8,128)(2,1)} async-done(((bf16[16,48,256]{2,1,0:T(8,128)(2,1)}), bf16[16,48,256]{2,1,0:T(8,128)(2,1)}, u32[]{:S(2)}, u32[]{:S(2)}) %all-to-all-start.4) | async-done | bytes 393248 | tf_op jit(solution)/shard_map/all_to_all | solution.py:116
  366.2 10.9 %all-to-all-start.3 = ((bf16[16,8,2816]{2,1,0:T(8,128)(2,1)}), bf16[16,8,2816]{2,1,0:T(8,128)(2,1)}, u32[]{:S(2)}, u32[]{:S(2)}) async-start(bf16[16,8,2816]{2,1,0:T(8,128)(2,1)} %broadcast_in_dim.14), calls=%async_computation.3 | async-start | bytes 1441792 | tf_op jit(solution)/shard_map/all_to_all | solution.py:94
  377.2 3.3 fusion.3
  380.5 3.2 convolution_add_fusion.2
  383.8 4.3 %fusion.2 = bf16[1,3,108,2048]{3,2,1,0:T(8,128)(2,1)} fusion(f32[3,108,2048]{2,1,0:T(8,128)S(1)} %convolution_add_fusion.2, f32[3,108,2048]{2,1,0:T(8,128)S(1)} %fusion.3, bf16[2048,2816]{1,0:T(8,128)(2,1)} %all-gather.3.cloned.1.call-done, bf16[3,108,256]{2,1,0:T(8,128)(2,1)S(1)} %copy-done.13, bf16[3,108,256]{2,1,0:T(8,128)(2,1)S(1)} %copy-done.9, ...), kind=kOutput, calls=%fused_computation.11 | convolution fusion | flops 1022699520 | bytes 10278912 | tf_op jit(solution)/shard_map/dot_general | solution.py:147
  389.1 19.0 %all-gather = bf16[768,256]{1,0:T(8,128)(2,1)S(1)} all-gather(bf16[48,256]{1,0:T(8,128)(2,1)S(1)} %reduce_sum.234), channel_id=2, replica_groups=mesh['strip_0'=8,'strip_1'=2,'sample_0'=4,'sample_1'=4] {'strip_0','stri..., dimensions={0}, use_global_device_ids=true | all-gather | bytes 417792 | tf_op jit(solution)/shard_map/all_gather | solution.py:132
  (120 shorter events, 38.7 us)
Async XLA Ops:
  7.2 2.2 copy-start.1
  7.2 98.5 %all-gather.3.cloned.1.call-start = ((), (), s32[]{:S(2)}) async-start(), calls=%async_computation.6 | async-start | bytes 12255232 | tf_op jit(solution)/shard_map/all_gather | solution.py:88
  10.3 38.4 %all-to-all-start = ((f32[16,1,2048]{2,1,0:T(1,128)}), f32[16,1,2048]{2,1,0:T(1,128)}, u32[]{:S(2)}, u32[]{:S(2)}) async-start(f32[16,1,2048]{2,1,0:T(1,128)} %broadcast_in_dim.10), calls=%async_computation | async-start | bytes 262144 | tf_op jit(solution)/shard_map/all_to_all | solution.py:94
  24.4 2.8 copy-start.16
  109.7 7.9 %copy-start = (bf16[2048,2816]{1,0:T(8,128)(2,1)S(1)}, bf16[2048,2816]{1,0:T(8,128)(2,1)}, u32[]{:S(2)}) copy-start(bf16[2048,2816]{1,0:T(8,128)(2,1)} %all-gather.3.cloned.1.call-done) | copy-start | bytes 34603012
  113.2 9.4 %collective-permute-start.1 = (bf16[3,108,256]{2,1,0:T(8,128)(2,1)S(1)}, bf16[3,108,256]{2,1,0:T(8,128)(2,1)S(1)}, u32[]{:S(2)}, u32[]{:S(2)}) collective-permute-start(bf16[3,108,256]{2,1,0:T(8,128)(2,1)S(1)} %fusion.51), channel_id=1, source_target_pairs={{0,64},{16,80},{32,96},{48,112},{64,128},{80,144},{96,160},{112,17... | collective-permute-start | bytes 497672 | tf_op jit(solution)/shard_map/ppermute | solution.py:106
  119.1 13.8 %collective-permute-start = (bf16[3,108,256]{2,1,0:T(8,128)(2,1)S(1)}, bf16[3,108,256]{2,1,0:T(8,128)(2,1)S(1)}, u32[]{:S(2)}, u32[]{:S(2)}) collective-permute-start(bf16[3,108,256]{2,1,0:T(8,128)(2,1)S(1)} %fusion.48), channel_id=1, source_target_pairs={{64,0},{80,16},{96,32},{112,48},{128,64},{144,80},{160,96},{176,11... | collective-permute-start | bytes 497672 | tf_op jit(solution)/shard_map/ppermute | solution.py:106
  122.4 92.0 %copy-start.2 = (f32[256,3,108]{0,2,1:T(8,128)}, f32[256,3,108]{0,2,1:T(8,128)S(1)}, u32[]{:S(2)}) copy-start(f32[256,3,108]{0,2,1:T(8,128)S(1)} %get-tuple-element.71) | copy-start | bytes 995332
  132.9 33.3 %copy-start.12 = (bf16[1,3,108,256]{3,2,1,0:T(8,128)(2,1)S(1)}, bf16[1,3,108,256]{3,2,1,0:T(8,128)(2,1)}, u32[]{:S(2)}) copy-start(bf16[1,3,108,256]{3,2,1,0:T(8,128)(2,1)} %param.11) | copy-start | bytes 497668
  199.8 27.8 %copy-start.6 = (bf16[3,108,256]{2,1,0:T(8,128)(2,1)}, bf16[3,108,256]{2,1,0:T(8,128)(2,1)S(1)}, u32[]{:S(2)}) copy-start(bf16[3,108,256]{2,1,0:T(8,128)(2,1)S(1)} %multiply_convert_fusion.2) | copy-start | bytes 497668
  199.8 28.7 %collective-permute-start.3 = (bf16[3,108,256]{2,1,0:T(8,128)(2,1)S(1)}, bf16[3,108,256]{2,1,0:T(8,128)(2,1)S(1)}, u32[]{:S(2)}, u32[]{:S(2)}) collective-permute-start(bf16[3,108,256]{2,1,0:T(8,128)(2,1)S(1)} %multiply_convert_fusion.2), channel_id=1, source_target_pairs={{0,64},{16,80},{32,96},{48,112},{64,128},{80,144},{96,160},{112,17... | collective-permute-start | bytes 497672 | tf_op jit(solution)/shard_map/ppermute | solution.py:106
  204.0 19.9 %collective-permute-start.2 = (bf16[3,108,256]{2,1,0:T(8,128)(2,1)S(1)}, bf16[3,108,256]{2,1,0:T(8,128)(2,1)S(1)}, u32[]{:S(2)}, u32[]{:S(2)}) collective-permute-start(bf16[3,108,256]{2,1,0:T(8,128)(2,1)S(1)} %multiply_convert_fusion.2), channel_id=1, source_target_pairs={{64,0},{80,16},{96,32},{112,48},{128,64},{144,80},{160,96},{176,11... | collective-permute-start | bytes 497672 | tf_op jit(solution)/shard_map/ppermute | solution.py:106
  205.9 15.6 %all-to-all-start.1 = ((f32[16,1,256]{2,1,0:T(1,128)}), f32[16,1,256]{2,1,0:T(1,128)S(1)}, u32[]{:S(2)}, u32[]{:S(2)}) async-start(f32[16,1,256]{2,1,0:T(1,128)} %broadcast_in_dim.12), calls=%async_computation.1 | async-start | bytes 32768 | tf_op jit(solution)/shard_map/all_to_all | solution.py:94
  214.2 121.7 %reduce-scatter.4.cloned.1.call-start = ((), (), s32[]{:S(2)}) async-start(), calls=%async_computation.7 | async-start | bytes 12255232 | tf_op jit(solution)/shard_map/reduce_scatter | solution.py:325
  223.9 9.6 %copy-start.4 = (bf16[3,108,256]{2,1,0:T(8,128)(2,1)}, bf16[3,108,256]{2,1,0:T(8,128)(2,1)S(1)}, u32[]{:S(2)}) copy-start(bf16[3,108,256]{2,1,0:T(8,128)(2,1)S(1)} %collective-permute-done.2) | copy-start | bytes 497668
  228.5 5.0 %copy-start.8 = (bf16[3,108,256]{2,1,0:T(8,128)(2,1)}, bf16[3,108,256]{2,1,0:T(8,128)(2,1)S(1)}, u32[]{:S(2)}) copy-start(bf16[3,108,256]{2,1,0:T(8,128)(2,1)S(1)} %collective-permute-done.3) | copy-start | bytes 497668
  335.9 17.0 %all-to-all-start.2 = ((bf16[16,8,2816]{2,1,0:T(8,128)(2,1)}), bf16[16,8,2816]{2,1,0:T(8,128)(2,1)S(1)}, u32[]{:S(2)}, u32[]{:S(2)}) async-start(bf16[16,8,2816]{2,1,0:T(8,128)(2,1)} %bitcast.175), calls=%async_computation.2 | async-start | bytes 1441792 | tf_op jit(solution)/shard_map/all_to_all | solution.py:116
  352.9 4.2 %copy-start.3 = (bf16[16,8,2816]{2,1,0:T(8,128)(2,1)}, bf16[16,8,2816]{2,1,0:T(8,128)(2,1)S(1)}, u32[]{:S(2)}) copy-start(bf16[16,8,2816]{2,1,0:T(8,128)(2,1)S(1)} %all-to-all-done.2) | copy-start | bytes 2162692
  352.9 12.5 %all-to-all-start.4 = ((bf16[16,48,256]{2,1,0:T(8,128)(2,1)}), bf16[16,48,256]{2,1,0:T(8,128)(2,1)}, u32[]{:S(2)}, u32[]{:S(2)}) async-start(bf16[16,48,256]{2,1,0:T(8,128)(2,1)} %bitcast.52), calls=%async_computation.4 | async-start | bytes 786432 | tf_op jit(solution)/shard_map/all_to_all | solution.py:116
  359.1 18.0 %copy-start.7 = (bf16[3,108,256]{2,1,0:T(8,128)(2,1)S(1)}, bf16[3,108,256]{2,1,0:T(8,128)(2,1)}, u32[]{:S(2)}) copy-start(bf16[3,108,256]{2,1,0:T(8,128)(2,1)} %copy-done.6) | copy-start | bytes 497668
  359.1 18.0 %copy-start.15 = (bf16[3,108,256]{2,1,0:T(8,128)(2,1)S(1)}, bf16[3,108,256]{2,1,0:T(8,128)(2,1)}, u32[]{:S(2)}) copy-start(bf16[3,108,256]{2,1,0:T(8,128)(2,1)} %get-tuple-element.52) | copy-start | bytes 497668
  366.2 42.6 %all-to-all-start.3 = ((bf16[16,8,2816]{2,1,0:T(8,128)(2,1)}), bf16[16,8,2816]{2,1,0:T(8,128)(2,1)}, u32[]{:S(2)}, u32[]{:S(2)}) async-start(bf16[16,8,2816]{2,1,0:T(8,128)(2,1)} %broadcast_in_dim.14), calls=%async_computation.3 | async-start | bytes 1441792 | tf_op jit(solution)/shard_map/all_to_all | solution.py:94
  377.1 3.3 copy-start.5
  377.1 3.3 copy-start.10
  377.2 3.3 copy-start.11
  380.5 3.3 copy-start.9
  380.5 3.3 copy-start.13
  380.5 3.3 copy-start.14
Sparse Core Ops, SparseCore 0:
  11.0 94.5 all-gather.2
  267.9 67.9 reduce-scatter.3

commit v2 on v0

v2 whole, which is shorter than its diff:
```python
import functools

import jax
import jax.numpy as jnp
from jax import lax
from jax.experimental import pallas as pl
from jax.experimental.pallas import tpu as pltpu
from jax.sharding import Mesh
from jax.sharding import PartitionSpec as P

RATE = 12
STRIP = ("strip_0", "strip_1")
SAMPLE = ("sample_0", "sample_1")
EPSILON = 1e-05
MESH_ID = pl.DeviceIdType.MESH
F32 = jnp.float32
BF16 = jnp.bfloat16

CHANS = 2048
FEAT = 256
HALF = 128
ROWS = 3
COLS = 108
PITCH = 112
BLOCK = ROWS * PITCH
SPOTS = 2 * BLOCK
TAPS = 10
WIDE = TAPS * HALF
WIDER = WIDE + HALF
SHARD = 128
SAMPLE_AREA = 48.0 * 108.0
TOTAL_AREA = 16.0 * SAMPLE_AREA
FACTOR = 1.0 / 16.0


def places():
    return tuple(lax.axis_index(a) for a in STRIP + SAMPLE)


def z_peer(z, k):
    return {"strip_0": lax.rem(z + k + 8, 8)}


def other_core(c):
    return {"strip_1": 1 - c}


def along(axis, y, x, d):
    if axis == "x":
        return {"sample_1": lax.rem(x + d + 4, 4)}
    return {"sample_0": lax.rem(y + d + 4, 4)}


def sample_peer(me, k):
    other = lax.rem(me + k, 16)
    return {"sample_0": lax.div(other, 4), "sample_1": lax.rem(other, 4)}


def strip_peer(me, k):
    other = lax.rem(me + k, 16)
    return {"strip_0": lax.div(other, 2), "strip_1": lax.rem(other, 2)}


def greet(peers):
    barrier = pltpu.get_barrier_semaphore()
    for peer in peers:
        pl.semaphore_signal(barrier, inc=1, device_id=peer, device_id_type=MESH_ID)
    pl.semaphore_wait(barrier, len(peers))


def push(src, dst, send, recv, peer):
    copy = pltpu.make_async_remote_copy(
        src_ref=src,
        dst_ref=dst,
        send_sem=send,
        recv_sem=recv,
        device_id=peer,
        device_id_type=MESH_ID,
    )
    copy.start()
    return copy


def spot_column(shape):
    full = lax.broadcasted_iota(jnp.int32, (shape[0] // PITCH, PITCH, shape[1]), 1)
    return full.reshape(shape)


def moved(values, offset, column):
    if offset == 0:
        return values
    spots = values.shape[0]
    if offset > 0:
        return jnp.where(column < COLS - offset, pltpu.roll(values, spots - offset, 0), 0.0)
    inside = (column >= -offset) & (column < COLS)
    return jnp.where(inside, pltpu.roll(values, -offset, 0), 0.0)


def ring_gather(full, y, x, send, recv):
    count = [0]
    sent = []

    def put(kind, a, b, part, first, d):
        if kind == 0:
            row = lax.rem(y + b + 4, 4) * 4 + lax.rem(x + a + 4, 4)
            axis = "x" if first else "y"
        else:
            row = lax.rem(y + a + 4, 4) * 4 + lax.rem(x + b + 4, 4)
            axis = "y" if first else "x"
        start, size = ((0, 64), (0, 32), (32, 32))[part]
        rows = pl.ds(pl.multiple_of(row * SHARD + kind * 64 + start, 32), size)
        k = count[0]
        count[0] += 1
        copy = push(full.at[rows, :], full.at[rows, :], send.at[k], recv.at[k], along(axis, y, x, d))
        sent.append(copy)
        return copy

    kinds = (0, 1)
    right, left, up, down = {}, {}, {}, {}
    fr, fl, fu, fd = {}, {}, {}, {}

    def spread(kind, a):
        up[kind, a] = put(kind, a, 0, 0, False, 1)
        down[kind, a] = put(kind, a, 0, 0, False, -1)

    def relay(kind, a):
        up[kind, a].wait_recv()
        fu[kind, a] = put(kind, a, -1, 1, False, 1)
        down[kind, a].wait_recv()
        fd[kind, a] = put(kind, a, 1, 2, False, -1)

    for kind in kinds:
        right[kind] = put(kind, 0, 0, 0, True, 1)
        left[kind] = put(kind, 0, 0, 0, True, -1)
    for kind in kinds:
        spread(kind, 0)
    for kind in kinds:
        right[kind].wait_recv()
        fr[kind] = put(kind, -1, 0, 1, True, 1)
        left[kind].wait_recv()
        fl[kind] = put(kind, 1, 0, 2, True, -1)
    for kind in kinds:
        spread(kind, -1)
        spread(kind, 1)
    for kind in kinds:
        relay(kind, 0)
    for kind in kinds:
        fr[kind].wait_recv()
        fl[kind].wait_recv()
        spread(kind, 2)
    for a in (-1, 1, 2):
        for kind in kinds:
            relay(kind, a)
    for a in (0, -1, 1, 2):
        for kind in kinds:
            fu[kind, a].wait_recv()
            fd[kind, a].wait_recv()
    return sent


def forward_kernel(
    images, w_point, w_atrous, w_image, w_proj,
    spots_ref, full_ref, proj_ref, point_ref, centre_ref, outer_ref, pooled_ref, image_ref,
    taps, pool_src, pool_slots,
    local, core_send, core_recv, ring_send, ring_recv, proj_send, proj_recv, pool_send, pool_recv,
):
    z, c, y, x = places()
    sample = y * 4 + x
    mine = pl.multiple_of(c * BLOCK, 16)
    spots_ref[pl.ds(mine, BLOCK), :] = jnp.zeros((BLOCK, CHANS), BF16)

    lane = pl.multiple_of(c * HALF, HALF)
    shard = pl.ds(pl.multiple_of(sample * SHARD, SHARD), SHARD)
    loads = [pltpu.make_async_copy(w_point.at[:, pl.ds(lane, HALF)], full_ref.at[shard, pl.ds(0, HALF)], local.at[0])]
    for t in range(9):
        loads.append(
            pltpu.make_async_copy(
                w_atrous.at[:, pl.ds(pl.multiple_of(t * FEAT + lane, HALF), HALF)],
                full_ref.at[shard, pl.ds((t + 1) * HALF, HALF)],
                local.at[t + 1],
            )
        )
    loads.append(
        pltpu.make_async_copy(w_image.at[:, pl.ds(lane, HALF)], full_ref.at[shard, pl.ds(WIDE, HALF)], local.at[10])
    )
    loads.append(pltpu.make_async_copy(w_proj, proj_ref.at[sample], local.at[11]))
    for load in loads:
        load.start()
    for r in range(ROWS):
        spots_ref[pl.ds(pl.multiple_of(mine + r * PITCH, 16), COLS), :] = images[r]
    greet(
        [along("x", y, x, 1), along("x", y, x, -1), along("y", y, x, 1), along("y", y, x, -1), other_core(c)]
        + [z_peer(z, k) for k in range(1, 8)]
        + [sample_peer(sample, k) for k in range(1, 16) ]
    )
    for load in loads:
        load.wait()
    to_core = push(
        spots_ref.at[pl.ds(mine, BLOCK), :], spots_ref.at[pl.ds(mine, BLOCK), :],
        core_send.at[0], core_recv.at[0], other_core(c),
    )
    sent = [
        push(proj_ref.at[sample], proj_ref.at[sample], proj_send.at[k - 1], proj_recv.at[k - 1], sample_peer(sample, k))
        for k in range(1, 16)
    ]
    received = list(sent)
    sent += ring_gather(full_ref, y, x, ring_send, ring_recv)
    to_core.wait()

    def add_rows(i, total):
        return total + spots_ref[pl.ds(pl.multiple_of(i * 16, 16), 16), :].astype(F32)

    sums = lax.fori_loop(0, SPOTS // 16, add_rows, jnp.zeros((16, CHANS), F32))
    pool_src[...] = jnp.sum(sums, axis=0, keepdims=True)
    pools = [
        push(pool_src, pool_slots.at[z], pool_send.at[k - 1], pool_recv.at[k - 1], z_peer(z, k)) for k in range(1, 8)
    ]
    pool_slots[z] = pool_src[...]

    def multiply(n, carry):
        product = jnp.dot(
            spots_ref[...],
            full_ref[:, pl.ds(pl.multiple_of(n * FEAT, FEAT), FEAT)],
            preferred_element_type=F32,
        )
        taps[2 * n] = product[:, :HALF]
        taps[2 * n + 1] = product[:, HALF:]
        return carry

    lax.fori_loop(0, TAPS // 2, multiply, 0)
    column = spot_column((SPOTS, HALF))
    point_ref[...] = taps[0]

    def row_tap(r):
        first = 1 + 3 * (r + 1)
        return taps[first + 1] + moved(taps[first], -RATE, column) + moved(taps[first + 2], RATE, column)

    centre_ref[...] = row_tap(0)
    outer_ref[0] = row_tap(-1).astype(BF16)
    outer_ref[1] = row_tap(1).astype(BF16)
    for copy in pools:
        copy.wait()
    pooled = (jnp.sum(pool_slots[...], axis=0) / SAMPLE_AREA).astype(BF16)
    pooled_ref[...] = pooled.astype(F32)
    image = jnp.dot(
        jnp.broadcast_to(pooled, (16, CHANS)), full_ref[:, pl.ds(WIDE, HALF)], preferred_element_type=F32
    )
    image_ref[...] = image[0:8]
    for copy in received:
        copy.wait_recv()
    for copy in sent:
        copy.wait_send()


def silu(v):
    return v * lax.logistic(v)


def silu_slope(v):
    s = lax.logistic(v)
    return s * (1.0 + v * (1.0 - s))


def middle_kernel(
    point_ref, centre_ref, outer_ref, image_ref, proj_ref, cotangent,
    result_ref, grad_point_ref, grad_atrous_ref, proj_part_ref, image_grad_ref,
    halo, cot, relu, result_send, result_half, mix, images, columns,
    ar_src, ar_mid, ar_z, ar_xy, cot_send, norm_p, norm_a,
    core_send, core_recv, halo_send, halo_recv, z_send, z_recv, xy_send, xy_recv,
):
    z, c, y, x = places()
    sample = y * 4 + x
    mine = pl.multiple_of(c * BLOCK, 16)
    theirs = pl.multiple_of((1 - c) * BLOCK, 16)
    lane = pl.multiple_of(c * HALF, HALF)
    other_lane = pl.multiple_of((1 - c) * HALF, HALF)
    mate = other_core(c)
    cot[pl.ds(mine, BLOCK), :] = jnp.zeros((BLOCK, HALF), BF16)
    cot_send[...] = jnp.zeros_like(cot_send)
    greet([mate] + [z_peer(z, k) for k in range(1, 8)] + [sample_peer(sample, k) for k in range(1, 16)])

    below = push(outer_ref.at[0], halo.at[0], halo_send.at[0], halo_recv.at[0], z_peer(z, 2))
    above = push(outer_ref.at[1], halo.at[1], halo_send.at[1], halo_recv.at[1], z_peer(z, -2))
    images[c] = image_ref[...]
    swap_image = push(image_ref, images.at[c], core_send.at[0], core_recv.at[0], mate)
    for r in range(ROWS):
        rows = pl.ds(r * PITCH, COLS)
        cot_send[rows, :] = cotangent[r, :, pl.ds(other_lane, HALF)]
        cot[pl.ds(pl.multiple_of(mine + r * PITCH, 16), COLS), :] = cotangent[r, :, pl.ds(lane, HALF)]
    swap_cot = push(cot_send, cot.at[pl.ds(mine, BLOCK), :], core_send.at[1], core_recv.at[1], mate)

    column = spot_column((SPOTS, HALF))
    inside = column < COLS

    def totals(i, rows):
        for k, row in enumerate(rows):
            ar_src[i, pl.ds(k, 1), :] = row
        copies = [
            push(ar_src.at[i], ar_z.at[i, z], z_send.at[i, k - 1], z_recv.at[i, k - 1], z_peer(z, k))
            for k in range(1, 8)
        ]
        ar_z[i, z] = ar_src[i]
        for copy in copies:
            copy.wait()
        whole = jnp.sum(ar_z[i], axis=0)
        ar_mid[i] = whole
        copies = [
            push(ar_mid.at[i], ar_xy.at[i, sample], xy_send.at[i, k - 1], xy_recv.at[i, k - 1], sample_peer(sample, k))
            for k in range(1, 16)
        ]
        ar_xy[i, sample] = whole
        for copy in copies:
            copy.wait()
        total = jnp.sum(ar_xy[i], axis=0)
        return [whole[k : k + 1] for k in range(4)], [total[k : k + 1] for k in range(4)]

    def down(v):
        return jnp.sum(v, axis=0, keepdims=True)

    below.wait()
    above.wait()
    point = point_ref[...]
    zero = jnp.zeros((SPOTS, HALF), F32)
    atrous = (
        centre_ref[...]
        + jnp.where(z >= 2, halo[0].astype(F32), zero)
        + jnp.where(z < 6, halo[1].astype(F32), zero)
    )
    _, (s0, s1, s2, s3) = totals(0, [down(point), down(point * point), down(atrous), down(atrous * atrous)])

    def finish(total, power):
        centre = total / TOTAL_AREA
        return centre, lax.rsqrt(power / TOTAL_AREA - centre * centre + EPSILON)

    centre_p, scale_p = finish(s0, s1)
    centre_a, scale_a = finish(s2, s3)
    norm_p[...] = (point - centre_p) * scale_p
    norm_a[...] = (atrous - centre_a) * scale_a
    relu[c, :, pl.ds(0, HALF)] = jnp.where(inside, silu(norm_p[...]), 0.0).astype(BF16)
    relu[c, :, pl.ds(HALF, HALF)] = jnp.where(inside, silu(norm_a[...]), 0.0).astype(BF16)
    swap_relu = push(relu.at[c], relu.at[c], core_send.at[4], core_recv.at[4], mate)

    swap_image.wait()
    halves = [images[0][0:1], images[1][0:1]]

    def mean_of(pair):
        return (jnp.sum(pair[0]) + jnp.sum(pair[1])) * (1.0 / FEAT)

    image_mean = mean_of(halves)
    apart = [h - image_mean for h in halves]
    layer_scale = lax.rsqrt(jnp.full((1, HALF), mean_of([a * a for a in apart]) + EPSILON, F32))
    layer_norm = [a * layer_scale for a in apart]
    relu_image = jnp.concatenate([silu(v) for v in layer_norm], axis=1).astype(BF16)
    image_row = jnp.dot(
        jnp.broadcast_to(relu_image, (16, FEAT)),
        proj_ref[pl.ds(2 * FEAT, FEAT), pl.ds(lane, HALF)],
        preferred_element_type=F32,
    )[0:1]
    swap_relu.wait()

    mixed = jnp.zeros((SPOTS, HALF), F32) + image_row
    for k in range(2):
        for b in range(2):
            mixed = mixed + jnp.dot(
                relu[k, :, pl.ds(b * HALF, HALF)],
                proj_ref[pl.ds(b * FEAT + k * HALF, HALF), pl.ds(lane, HALF)],
                preferred_element_type=F32,
            )
    mixed = jnp.where(inside, mixed, 0.0)
    (mixed_sample, _, _, _), (s0, s1, _, _) = totals(1, [down(mixed), down(mixed * mixed), down(mixed[0:8]), down(mixed[0:8])])
    centre_m, scale_m = finish(s0, s1)
    norm_mix = (mixed - centre_m) * scale_m
    result = silu(norm_mix).astype(BF16)
    result_send[0] = result[:BLOCK]
    result_send[1] = result[BLOCK:]
    swap_result = push(result_send.at[1 - c], result_half, core_send.at[5], core_recv.at[5], mate)
    swap_cot.wait()
    upstream = jnp.where(inside, cot[...].astype(F32) * silu_slope(norm_mix), 0.0)
    (up_sample, _, _, _), (s0, s1, _, _) = totals(
        2, [down(upstream), down(upstream * norm_mix), down(mixed[0:8]), down(mixed[0:8])]
    )
    mean_u = s0 / TOTAL_AREA
    mean_un = s1 / TOTAL_AREA
    grad_mix = jnp.where(inside, (upstream - mean_u - norm_mix * mean_un) * scale_m, 0.0)
    mix[c] = grad_mix.astype(BF16)
    norm_sample = (mixed_sample - SAMPLE_AREA * centre_m) * scale_m
    column_total = (up_sample - SAMPLE_AREA * mean_u - mean_un * norm_sample) * scale_m
    columns[c] = jnp.broadcast_to(column_total, (8, HALF))
    swap_mix = push(mix.at[c], mix.at[c], core_send.at[6], core_recv.at[6], mate)
    swap_columns = push(columns.at[c], columns.at[c], core_send.at[7], core_recv.at[7], mate)
    swap_mix.wait()
    swap_columns.wait()

    def back(first):
        total = None
        for k in range(2):
            term = lax.dot_general(
                mix[k],
                proj_ref[pl.ds(pl.multiple_of(first + lane, HALF), HALF), pl.ds(k * HALF, HALF)],
                (((1,), (1,)), ((), ())),
                preferred_element_type=F32,
            )
            total = term if total is None else total + term
        return total

    norm_point = norm_p[...]
    norm_atrous = norm_a[...]
    up_point = back(0) * silu_slope(norm_point)
    up_atrous = back(FEAT) * silu_slope(norm_atrous)
    _, (s0, s1, s2, s3) = totals(
        3, [down(up_point), down(up_point * norm_point), down(up_atrous), down(up_atrous * norm_atrous)]
    )

    def back_norm(up, norm, first, second, scale):
        grad = (up - first / TOTAL_AREA - norm * (second / TOTAL_AREA)) * scale
        return jnp.where(inside, grad, 0.0).astype(BF16)

    grad_point_ref[...] = back_norm(up_point, norm_point, s0, s1, scale_p)
    grad_atrous_ref[...] = back_norm(up_atrous, norm_atrous, s2, s3, scale_a)

    column_b = jnp.concatenate([columns[0][0:1], columns[1][0:1]], axis=1).astype(BF16)
    back_image = lax.dot_general(
        jnp.broadcast_to(column_b, (16, FEAT)),
        proj_ref[pl.ds(2 * FEAT, FEAT), :],
        (((1,), (1,)), ((), ())),
        preferred_element_type=F32,
    )
    up_image = [back_image[0:1, k * HALF : (k + 1) * HALF] * silu_slope(layer_norm[k]) for k in range(2)]
    mean_up = mean_of(up_image)
    mean_up_norm = mean_of([up_image[k] * layer_norm[k] for k in range(2)])
    image_grad = jnp.concatenate(
        [(up_image[k] - mean_up - layer_norm[k] * mean_up_norm) * layer_scale for k in range(2)], axis=1
    )
    image_grad_ref[...] = jnp.broadcast_to(image_grad.astype(BF16).astype(F32), (8, FEAT))

    for k in range(2):
        part = lax.dot_general(
            relu[k], mix[c], (((0,), (0,)), ((), ())), preferred_element_type=F32
        ) * FACTOR
        proj_part_ref[pl.ds(k * HALF, HALF), :] = part[:HALF].astype(BF16)
        proj_part_ref[pl.ds(FEAT + k * HALF, HALF), :] = part[HALF:].astype(BF16)
    once = lax.broadcasted_iota(jnp.int32, (16, FEAT), 0) == 0
    gate = jnp.where(z == 0, FACTOR, 0.0).astype(F32)
    outer = lax.dot_general(
        jnp.where(once, jnp.broadcast_to(relu_image.astype(F32), (16, FEAT)), 0.0).astype(BF16),
        jnp.broadcast_to(columns[c][0:1], (16, HALF)).astype(BF16),
        (((0,), (0,)), ((), ())),
        preferred_element_type=F32,
    )
    proj_part_ref[pl.ds(2 * FEAT, FEAT), :] = (outer * gate).astype(BF16)

    swap_result.wait()
    own = result_send[c]
    came = result_half[...]
    for r in range(ROWS):
        rows = slice(r * PITCH, r * PITCH + COLS)
        result_ref[r, :, pl.ds(lane, HALF)] = own[rows]
        result_ref[r, :, pl.ds(other_lane, HALF)] = came[rows]


def backward_kernel(
    spots_ref, full_ref, pooled_ref, grad_point_ref, grad_atrous_ref, proj_part_ref, image_grad_ref,
    input_grad_ref, out_point_ref, out_atrous_ref, out_image_ref, out_proj_ref,
    halo, cols, partial, opposite, beside, pair, own, away, came,
    z_slots, z_sum, joined, proj_slots, proj_sum, proj_all, pool_rows, pool_all, image_all,
    halo_send, halo_recv, ring_send, ring_recv, core_send, core_recv,
    z_send, z_recv, all_send, all_recv, proj_send, proj_recv, spread_send, spread_recv,
    pool_send, pool_recv, image_send, image_recv,
):
    z, c, y, x = places()
    sample = y * 4 + x
    strip = z * 2 + c
    mate = other_core(c)
    greet([strip_peer(strip, k) for k in range(1, 16)] + [sample_peer(sample, k) for k in range(1, 16)])
    upper = push(grad_atrous_ref, halo.at[1], halo_send.at[1], halo_recv.at[1], z_peer(z, 2))
    lower = push(grad_atrous_ref, halo.at[0], halo_send.at[0], halo_recv.at[0], z_peer(z, -2))

    def to_samples(src_of, slots, send, recv):
        return [
            push(
                src_of(lax.rem(sample + k, 16)), slots.at[sample], send.at[k - 1], recv.at[k - 1],
                sample_peer(sample, k),
            )
            for k in range(1, 16)
        ]

    for k in range(16):
        pool_rows[k] = jnp.broadcast_to(pooled_ref[:, k * SHARD : (k + 1) * SHARD], (8, SHARD))
    sends = to_samples(lambda j: pool_rows.at[j], pool_all, pool_send, pool_recv)
    sends += to_samples(lambda j: image_grad_ref, image_all, image_send, image_recv)
    proj_copies = to_samples(lambda j: proj_part_ref.at[j], proj_slots, proj_send, proj_recv)
    pool_all[sample] = pool_rows[sample]
    image_all[sample] = image_grad_ref[...]
    proj_slots[sample] = proj_part_ref[sample]

    column = spot_column((SPOTS, HALF))
    cols[:, pl.ds(0, HALF)] = grad_point_ref[...]

    def fill(r, source):
        for s in (-1, 0, 1):
            t = 1 + 3 * (r + 1) + (s + 1)
            cols[:, pl.ds(t * HALF, HALF)] = moved(source, -RATE * s, column).astype(BF16)

    fill(0, grad_atrous_ref[...].astype(F32))
    zero = jnp.zeros((SPOTS, HALF), F32)
    upper.wait()
    lower.wait()
    fill(1, jnp.where(z >= 2, halo[1].astype(F32), zero))
    fill(-1, jnp.where(z < 6, halo[0].astype(F32), zero))

    def weight_part(k, carry):
        at = pl.ds(pl.multiple_of(k * FEAT, FEAT), FEAT)
        part = lax.dot_general(
            spots_ref[:, at], cols[...], (((0,), (0,)), ((), ())), preferred_element_type=F32
        )
        partial[at, :] = (part * FACTOR).astype(BF16)
        return carry

    lax.fori_loop(0, CHANS // FEAT, weight_part, 0)

    count = [0]
    done = []

    class Ring:
        def __init__(self, slot, axis, base, index):
            self.slot, self.axis, self.base, self.index = slot, axis, base, index

        def rows(self, o, start, size):
            return pl.ds(pl.multiple_of(self.index(o) * SHARD + self.base + start, 32), size)

        def put(self, src, dst, d):
            k = count[0]
            count[0] += 1
            copy = push(src, dst, ring_send.at[k], ring_recv.at[k], along(self.axis, y, x, d))
            done.append(copy)
            return copy

        def far(self):
            s = self.slot
            self.m0 = self.put(partial.at[self.rows(2, 0, 32), :], opposite.at[s, 0], 1)
            self.m1 = self.put(partial.at[self.rows(2, 32, 32), :], opposite.at[s, 1], -1)

        def near(self):
            s = self.slot
            self.m2 = self.put(partial.at[self.rows(1, 32, 32), :], beside.at[s, 0, pl.ds(32, 32), :], 1)
            self.m3 = self.put(partial.at[self.rows(-1, 0, 32), :], beside.at[s, 1, pl.ds(0, 32), :], -1)

        def relay(self):
            s = self.slot
            self.m0.wait_recv()
            at = self.rows(1, 0, 32)
            partial[at, :] = (partial[at, :].astype(F32) + opposite[s, 0].astype(F32)).astype(BF16)
            self.m4 = self.put(partial.at[at, :], beside.at[s, 0, pl.ds(0, 32), :], 1)
            self.m1.wait_recv()
            at = self.rows(-1, 32, 32)
            partial[at, :] = (partial[at, :].astype(F32) + opposite[s, 1].astype(F32)).astype(BF16)
            self.m5 = self.put(partial.at[at, :], beside.at[s, 1, pl.ds(32, 32), :], -1)

        def close(self):
            s = self.slot
            for m in (self.m2, self.m3, self.m4, self.m5):
                m.wait_recv()
            at = self.rows(0, 0, 64)
            partial[at, :] = (
                partial[at, :].astype(F32) + beside[s, 0].astype(F32) + beside[s, 1].astype(F32)
            ).astype(BF16)

    def block(dy, dx):
        return lax.rem(y + dy + 4, 4) * 4 + lax.rem(x + dx + 4, 4)

    order = (2, 1, -1, 0)
    rings = []
    for n, a in enumerate(order):
        rings.append(Ring(n, "y", 0, functools.partial(lambda a, o: block(o, a), a)))
        rings.append(Ring(4 + n, "x", 64, functools.partial(lambda a, o: block(a, o), a)))
    last = [
        Ring(8, "x", 0, lambda o: block(0, o)),
        Ring(9, "y", 64, lambda o: block(o, 0)),
    ]
    for ring in rings:
        ring.far()
    for ring in rings:
        ring.near()

    half_grad = image_grad_ref[:, pl.ds(pl.multiple_of(c * HALF, HALF), HALF)]
    grad_rows = jnp.concatenate([half_grad, half_grad], axis=0).astype(BF16)
    core_copies = []
    def input_part(k, carry):
        at = pl.ds(pl.multiple_of(k * FEAT, FEAT), FEAT)
        part = lax.dot_general(
            cols[...], full_ref[at, pl.ds(0, WIDE)], (((1,), (1,)), ((), ())), preferred_element_type=F32
        )
        pool = lax.dot_general(
            grad_rows, full_ref[at, pl.ds(WIDE, HALF)], (((1,), (1,)), ((), ())), preferred_element_type=F32
        )[0:1] / SAMPLE_AREA
        part = part + pool
        pair[0] = part[:BLOCK]
        pair[1] = part[BLOCK:]
        own[k] = pair[c]
        away[k] = pair[1 - c].astype(BF16)
        return carry

    lax.fori_loop(0, CHANS // FEAT, input_part, 0)
    swap = push(away, came, core_send.at[0], core_recv.at[0], mate)

    for ring in rings:
        ring.relay()
    for n in range(4):
        for ring in (rings[2 * n], rings[2 * n + 1]):
            ring.close()
        if n == 0:
            for ring in last:
                ring.far()
        if n == 2:
            for ring in last:
                ring.near()
    for ring in last:
        ring.relay()

    swap.wait()
    for k in range(CHANS // FEAT):
        total = (own[k] + came[k].astype(F32)).astype(BF16)
        for r in range(ROWS):
            input_grad_ref[r, :, pl.ds(k * FEAT, FEAT)] = total[r * PITCH : r * PITCH + COLS]

    for copy in sends:
        copy.wait()
    pools = pool_all[...][:, 0, :].astype(BF16)
    grads = image_all[...][:, 0, :].astype(BF16)
    out_image_ref[...] = (
        lax.dot_general(pools, grads, (((0,), (0,)), ((), ())), preferred_element_type=F32) * FACTOR
    )
    for copy in proj_copies:
        copy.wait()
    proj_sum[...] = jnp.sum(proj_slots[...].astype(F32), axis=0).astype(BF16)

    def to_strips(src, dst, send, recv):
        return [push(src, dst, send.at[k - 1], recv.at[k - 1], strip_peer(strip, k)) for k in range(1, 16)]

    spread = to_strips(proj_sum, proj_all.at[strip], spread_send, spread_recv)
    proj_all[strip] = proj_sum[...]

    for ring in last:
        ring.close()
    here = sample * SHARD
    z_copies = [
        push(
            partial.at[pl.ds(pl.multiple_of(here + lax.rem(z + k, 8) * 16, 16), 16), :],
            z_slots.at[z], z_send.at[k - 1], z_recv.at[k - 1], z_peer(z, k),
        )
        for k in range(1, 8)
    ]
    z_slots[z] = partial[pl.ds(pl.multiple_of(here + z * 16, 16), 16), :]
    for copy in z_copies:
        copy.wait()
    z_sum[...] = jnp.sum(z_slots[...].astype(F32), axis=0).astype(BF16)
    my_rows = pl.ds(pl.multiple_of(z * 16, 16), 16)
    all_copies = to_strips(z_sum, joined.at[c, my_rows, :], all_send, all_recv)
    joined[c, my_rows, :] = z_sum[...]
    for copy in spread:
        copy.wait()
    for k in range(2):
        total = proj_all[k].astype(F32)
        for level in range(1, 8):
            total = total + proj_all[2 * level + k].astype(F32)
        out_proj_ref[:, pl.ds(k * HALF, HALF)] = total
    for copy in all_copies:
        copy.wait()
    for k in range(2):
        out_point_ref[:, pl.ds(k * HALF, HALF)] = joined[k, :, pl.ds(0, HALF)].astype(F32)
        for t in range(9):
            out_atrous_ref[:, pl.ds(t * FEAT + k * HALF, HALF)] = joined[k, :, pl.ds((t + 1) * HALF, HALF)].astype(F32)
    for copy in done:
        copy.wait_send()


VMEM = pl.BlockSpec(memory_space=pltpu.VMEM)
ANY = pl.BlockSpec(memory_space=pl.ANY)


def dma(*shape):
    return pltpu.SemaphoreType.DMA(shape)


def sized(dtype, *shape):
    return jax.ShapeDtypeStruct(shape, dtype)


def params(call_id, mib):
    return pltpu.CompilerParams(collective_id=call_id, has_side_effects=True, vmem_limit_bytes=mib << 20)


def on_device(images, w_point, w_atrous, w_image, w_proj, cotangent):
    spots, full, proj, point, centre, outer, pooled, image = pl.pallas_call(
        forward_kernel,
        out_shape=[
            sized(BF16, SPOTS, CHANS),
            sized(BF16, CHANS, WIDER),
            sized(BF16, 16, 48, FEAT),
            sized(F32, SPOTS, HALF),
            sized(F32, SPOTS, HALF),
            sized(BF16, 2, SPOTS, HALF),
            sized(F32, 1, CHANS),
            sized(F32, 8, HALF),
        ],
        in_specs=[VMEM] + [ANY] * 4,
        out_specs=[VMEM] * 8,
        scratch_shapes=[
            pltpu.VMEM((TAPS, SPOTS, HALF), F32),
            pltpu.VMEM((1, CHANS), F32),
            pltpu.VMEM((8, 1, CHANS), F32),
            dma(15), dma(1), dma(1), dma(40), dma(40), dma(15), dma(15), dma(7), dma(7),
        ],
        compiler_params=params(0, 48),
        name="forward_gather",
    )(images[0], w_point, w_atrous, w_image, w_proj)

    result, grad_point, grad_atrous, proj_part, image_grad = pl.pallas_call(
        middle_kernel,
        out_shape=[
            sized(BF16, ROWS, COLS, FEAT),
            sized(BF16, SPOTS, HALF),
            sized(BF16, SPOTS, HALF),
            sized(BF16, 3 * FEAT, HALF),
            sized(F32, 8, FEAT),
        ],
        in_specs=[VMEM] * 6,
        out_specs=[VMEM] * 5,
        scratch_shapes=[
            pltpu.VMEM((2, SPOTS, HALF), BF16),
            pltpu.VMEM((SPOTS, HALF), BF16),
            pltpu.VMEM((2, SPOTS, FEAT), BF16),
            pltpu.VMEM((2, BLOCK, HALF), BF16),
            pltpu.VMEM((BLOCK, HALF), BF16),
            pltpu.VMEM((2, SPOTS, HALF), BF16),
            pltpu.VMEM((2, 8, HALF), F32),
            pltpu.VMEM((2, 8, HALF), F32),
            pltpu.VMEM((4, 4, HALF), F32),
            pltpu.VMEM((4, 4, HALF), F32),
            pltpu.VMEM((4, 8, 4, HALF), F32),
            pltpu.VMEM((4, 16, 4, HALF), F32),
            pltpu.VMEM((BLOCK, HALF), BF16),
            pltpu.VMEM((SPOTS, HALF), F32),
            pltpu.VMEM((SPOTS, HALF), F32),
            dma(8), dma(8), dma(2), dma(2), dma(4, 7), dma(4, 7), dma(4, 15), dma(4, 15),
        ],
        compiler_params=params(1, 32),
        name="middle",
    )(point, centre, outer, image, proj.reshape(3 * FEAT, FEAT), cotangent[0])

    input_grad, g_point, g_atrous, g_image, g_proj = pl.pallas_call(
        backward_kernel,
        out_shape=[
            sized(BF16, ROWS, COLS, CHANS),
            sized(F32, SHARD, FEAT),
            sized(F32, SHARD, 9 * FEAT),
            sized(F32, SHARD, FEAT),
            sized(F32, 48, FEAT),
        ],
        in_specs=[VMEM] * 7,
        out_specs=[VMEM] * 5,
        scratch_shapes=[
            pltpu.VMEM((2, SPOTS, HALF), BF16),
            pltpu.VMEM((SPOTS, WIDE), BF16),
            pltpu.VMEM((CHANS, WIDE), BF16),
            pltpu.VMEM((10, 2, 32, WIDE), BF16),
            pltpu.VMEM((10, 2, 64, WIDE), BF16),
            pltpu.VMEM((2, BLOCK, FEAT), F32),
            pltpu.VMEM((8, BLOCK, FEAT), F32),
            pltpu.VMEM((8, BLOCK, FEAT), BF16),
            pltpu.VMEM((8, BLOCK, FEAT), BF16),
            pltpu.VMEM((8, 16, WIDE), BF16),
            pltpu.VMEM((16, WIDE), BF16),
            pltpu.VMEM((2, SHARD, WIDE), BF16),
            pltpu.VMEM((16, 48, HALF), BF16),
            pltpu.VMEM((48, HALF), BF16),
            pltpu.VMEM((16, 48, HALF), BF16),
            pltpu.VMEM((16, 8, SHARD), F32),
            pltpu.VMEM((16, 8, SHARD), F32),
            pltpu.VMEM((16, 8, FEAT), F32),
            dma(2), dma(2), dma(60), dma(60), dma(1), dma(1), dma(7), dma(7), dma(15), dma(15),
            dma(15), dma(15), dma(15), dma(15), dma(15), dma(15), dma(15), dma(15),
        ],
        compiler_params=params(2, 56),
        name="backward_reduce",
    )(spots, full, pooled, grad_point, grad_atrous, proj_part.reshape(16, 48, HALF), image_grad)
    return (result[None], input_grad[None], g_point, g_atrous, g_image, g_proj)


def solution(mesh):
    finer = Mesh(mesh.devices.reshape(8, 2, 4, 4), STRIP + SAMPLE)
    placed = (
        P(SAMPLE, STRIP, None, None),
        P(SAMPLE, None),
        P(SAMPLE, None),
        P(SAMPLE, None),
        P(SAMPLE, None),
        P(SAMPLE, STRIP, None, None),
    )
    return jax.shard_map(
        on_device,
        mesh=finer,
        in_specs=placed,
        out_specs=(
            P(SAMPLE, STRIP, None, None),
            P(SAMPLE, STRIP, None, None),
            P(SAMPLE, None),
            P(SAMPLE, None),
            P(SAMPLE, None),
            P(SAMPLE, None),
        ),
        check_vma=False,
    )
```

time: 487 us -> 209 us (0.43)
  Pallas kernels: 0 us -> 195 us
  blocking collectives: 180 us -> 0 us
  waiting for transfers between devices: 135 us -> 0 us
  starting transfers between devices: 55.3 us -> 0 us
  matrix products: 34.6 us -> 0 us
  other arithmetic: 25.1 us -> 0 us
  local copies, waits for them, and re-layouts: 38.2 us -> 13.7 us
  between operations: 17.3 us -> 0.71 us
    pallas_call x0 -> x3, Pallas kernels: none -> 195 us  [the longest x1 83.3 us: on_device(): pl.pallas_call(backward_kernel, out_shape=[sized(BF16, ROWS, COLS, CHANS)...]
    psum x16 -> x0, blocking collectives: 140 us -> none  [one_axis_at_a_time(): array = lax.psum(array, axis)]
    reduce_scatter x1 -> x0, waiting for transfers between devices: 67.2 us -> none  [on_device(): lax.psum_scatter(jnp.concatenate([tap_terms, swapped_pool[:, None] * imag...]
    all_gather x1 -> x0, waiting for transfers between devices: 49.2 us -> none  [side_by_side(): filled = lax.all_gather(both, axis, axis=dim, tiled=True)]
    all_to_all x5 -> x0, starting transfers between devices: 45.3 us -> none  [the longest x3 34.7 us: from_everyone(): lax.all_to_all(jnp.broadcast_to(array[None], (peers, *array.shape)), axis...]
    all_gather x2 -> x0, blocking collectives: 39.7 us -> none  [the longest x1 20.7 us: on_device(): lax.all_gather(w_proj, SAMPLE, axis=0, tiled=True)]
    dot_general x16 -> x0, matrix products: 34.6 us -> none  [the longest x7 15.7 us: contract_last(): lax.dot_general(left, right, (((left.ndim - 1,), (1,)), ((), ())), prefer...]
    all_to_all x5 -> x0, waiting for transfers between devices: 19 us -> none  [the longest x2 12.8 us: sum_at_owner(): lax.all_to_all(tiles, axis, split_axis=0, concat_axis=0, tiled=True)]
  transfers between devices with their start and end apart: 11 -> 0, of which waited for: 5 -> 0; matrix products, arithmetic and copies ran while one was open for 9% -> 0% of each run, Pallas kernels for 0% -> 0%
where the time goes in v2:
time: 209 us
  Pallas kernels  195 us (93%)
  local copies, waits for them, and re-layouts  13.7 us (7%)
    pallas_call x1, Pallas kernels, on_device(): pl.pallas_call(backward_kernel, out_shape=[sized(BF16, ROWS, COLS, CHANS)...  83.3 us
    pallas_call x1, Pallas kernels, on_device(): pl.pallas_call(forward_kernel, out_shape=[sized(BF16, SPOTS, CHANS), size...  55.7 us
    pallas_call x1, Pallas kernels, on_device(): pl.pallas_call(middle_kernel, out_shape=[sized(BF16, ROWS, COLS, FEAT), s...  55.5 us
    unnamed x36, local copies, waits for them, and re-layouts  13.7 us

profile of v2, /device:TPU:1, one launch (start us, length us, event | category | flops | bytes accessed | tf_op | source)
XLA Modules:
  0.0 209.0 jit_solution(3610121931212250331)
XLA Ops:
  0.6 0.0 copy-start
  0.6 1.3 copy-done
  2.0 0.0 copy-start.1
  2.0 1.1 copy-done.1
  3.0 0.0 copy-start.6
  3.0 0.8 copy-done.6
  3.9 0.0 copy-start.7
  3.9 0.8 copy-done.7
  4.7 0.0 copy-start.8
  4.7 0.7 copy-done.8
  5.5 0.0 copy-start.3
  5.5 55.7 %forward_gather.1 = (bf16[672,2048]{1,0:T(8,128)(2,1)}, bf16[2048,1408]{1,0:T(8,128)(2,1)}, bf16[16,48,256]{2,1,0:T(8,128)(2,1)S(1)}, f32[672,128]{1,0:T(8,128)S...) custom-call(bf16[3,108,2048]{2,1,0:T(8,128)(2,1)S(1)} %bitcast.6, ...), custom_call_target="tpu_custom_call" | custom-call | tf_op jit(solution)/shard_map/forward_gather/pallas_call | solution.py:694
  61.2 0.0 copy-start.9
  61.2 0.0 copy-done.3
  61.2 55.5 %middle.1 = (bf16[3,108,256]{2,1,0:T(8,128)(2,1)S(1)}, bf16[672,128]{1,0:T(8,128)(2,1)S(1)}, bf16[672,128]{1,0:T(8,128)(2,1)S(1)}, bf16[768,128]{1,0:T(8,128)(2,1)S(1)}, f32[8,256]{1,0:T(8,128)S(1)}) custom-call(f32[672,128]{1,0:T(8,128)S(1)} %get-tuple-element.24.point_ref, f32[672,128]{1,0:T(8,128)S(1)} %get-tuple-element.25.centre_ref, ...), custom_call_target="tpu_custom_call" | custom-call | tf_op jit(solution)/shard_map/middle/pallas_call | solution.py:718
  116.7 0.0 copy-done.9
  116.7 0.0 copy-start.2
  116.7 0.7 copy-done.2
  117.4 0.7 copy-done.4
  118.1 0.7 copy-done.5
  118.7 0.6 copy-done.10
  119.3 83.3 %backward_reduce.1 = (bf16[3,108,2048]{2,1,0:T(8,128)(2,1)}, f32[128,256]{1,0:T(8,128)}, f32[128,2304]{1,0:T(8,128)}, f32[128,256]{1,0:T(8,128)}, f32[48,256]{1,0:T(8,128)}) custom-call(bf16[672,2048]{1,0:T(8,128)(2,1)} %get-tuple-element.30.spots_ref, bf16[2048,1408]{1,0:T(8,128)(2,1)} %get-tuple-element.31.full_ref, f32[1,2048]{1,0:T(1,128)} %copy-done.9, ...), custom_call_target="tpu_custom_call" | custom-call | tf_op jit(solution)/shard_map/backward_reduce/pallas_call | solution.py:751
  202.6 0.7 copy.18
  203.3 2.7 %copy.19 = bf16[1,3,108,2048]{3,2,1,0:T(8,128)(2,1)} copy(bf16[1,3,108,2048]{3,2,1,0:T(8,128)(2,1)} %bitcast.11) | data formatting | bytes 2654208
  206.0 0.0 copy-done.13
  206.0 0.7 copy.20
  206.7 0.0 copy-done.11
  206.7 1.0 copy.21
  207.7 0.0 copy-done.12
  207.7 0.7 copy.22
  208.3 0.0 copy-done.14
  208.3 0.6 copy.23
  (7 shorter events, 0.0 us)
Async XLA Ops:
  0.6 1.3 copy-start
  2.0 1.1 copy-start.1
  3.0 0.8 copy-start.6
  3.9 0.8 copy-start.7
  4.7 0.7 copy-start.8
  5.5 55.8 %copy-start.3 = (bf16[1,3,108,256]{3,2,1,0:T(8,128)(2,1)S(1)}, bf16[1,3,108,256]{3,2,1,0:T(8,128)(2,1)}, u32[]{:S(2)}) copy-start(bf16[1,3,108,256]{3,2,1,0:T(8,128)(2,1)} %param.11) | copy-start | bytes 497668
  61.2 55.5 %copy-start.9 = (f32[1,2048]{1,0:T(1,128)}, f32[1,2048]{1,0:T(1,128)S(1)}, u32[]{:S(2)}) copy-start(f32[1,2048]{1,0:T(1,128)S(1)} %get-tuple-element.32.pooled_ref) | copy-start | bytes 24580
  116.7 0.7 copy-start.2
  117.4 0.7 copy-start.4
  118.1 0.7 copy-start.5
  118.7 0.6 copy-start.10
  203.3 2.7 %copy-start.13 = (f32[128,256]{1,0:T(8,128)S(1)}, f32[128,256]{1,0:T(8,128)}, u32[]{:S(2)}) copy-start(f32[128,256]{1,0:T(8,128)} %get-tuple-element.50) | copy-start | bytes 393220
  203.3 3.3 %copy-start.11 = (f32[128,2304]{1,0:T(8,128)S(1)}, f32[128,2304]{1,0:T(8,128)}, u32[]{:S(2)}) copy-start(f32[128,2304]{1,0:T(8,128)} %get-tuple-element.51) | copy-start | bytes 3538948
  206.0 1.7 copy-start.12
  206.7 1.7 copy-start.14

commit v3 on v2

v3 whole, which is shorter than its diff:
```python
import functools
import types

import jax
import jax.numpy as jnp
from jax import lax
from jax.experimental import pallas as pl
from jax.experimental.pallas import tpu as pltpu
from jax.sharding import Mesh
from jax.sharding import PartitionSpec as P

RATE = 12
STRIP = ("strip_0", "strip_1")
SAMPLE = ("sample_0", "sample_1")
EPSILON = 1e-05
MESH_ID = pl.DeviceIdType.MESH
F32 = jnp.float32
BF16 = jnp.bfloat16

CHANS = 2048
FEAT = 256
HALF = 128
ROWS = 3
COLS = 108
PITCH = 112
BLOCK = ROWS * PITCH
SPOTS = 2 * BLOCK
TAPS = 10
WIDE = TAPS * HALF
WIDER = WIDE + HALF
SHARD = 128
SAMPLE_AREA = 48.0 * 108.0
TOTAL_AREA = 16.0 * SAMPLE_AREA
FACTOR = 1.0 / 16.0


def places():
    return tuple(lax.axis_index(a) for a in STRIP + SAMPLE)


def z_peer(z, k):
    return {"strip_0": lax.rem(z + k + 8, 8)}


def other_core(c):
    return {"strip_1": 1 - c}


def along(axis, y, x, d):
    if axis == "x":
        return {"sample_1": lax.rem(x + d + 4, 4)}
    return {"sample_0": lax.rem(y + d + 4, 4)}


def sample_peer(me, k):
    other = lax.rem(me + k, 16)
    return {"sample_0": lax.div(other, 4), "sample_1": lax.rem(other, 4)}


def strip_peer(me, k):
    other = lax.rem(me + k, 16)
    return {"strip_0": lax.div(other, 2), "strip_1": lax.rem(other, 2)}


def greet(peers):
    barrier = pltpu.get_barrier_semaphore()
    for peer in peers:
        pl.semaphore_signal(barrier, inc=1, device_id=peer, device_id_type=MESH_ID)
    pl.semaphore_wait(barrier, len(peers))


def push(src, dst, send, recv, peer):
    copy = pltpu.make_async_remote_copy(
        src_ref=src,
        dst_ref=dst,
        send_sem=send,
        recv_sem=recv,
        device_id=peer,
        device_id_type=MESH_ID,
    )
    copy.start()
    return copy


def spot_column(shape):
    full = lax.broadcasted_iota(jnp.int32, (shape[0] // PITCH, PITCH, shape[1]), 1)
    return full.reshape(shape)


def moved(values, offset, column):
    if offset == 0:
        return values
    spots = values.shape[0]
    if offset > 0:
        return jnp.where(column < COLS - offset, pltpu.roll(values, spots - offset, 0), 0.0)
    inside = (column >= -offset) & (column < COLS)
    return jnp.where(inside, pltpu.roll(values, -offset, 0), 0.0)


def ring_gather(full, y, x, send, recv, early, late):
    count = [0]
    sent = []

    def put(kind, a, b, part, first, d):
        if kind == 0:
            row = lax.rem(y + b + 4, 4) * 4 + lax.rem(x + a + 4, 4)
            axis = "x" if first else "y"
        else:
            row = lax.rem(y + a + 4, 4) * 4 + lax.rem(x + b + 4, 4)
            axis = "y" if first else "x"
        start, size = ((0, 64), (0, 32), (32, 32))[part]
        rows = pl.ds(pl.multiple_of(row * SHARD + kind * 64 + start, 32), size)
        k = count[0]
        count[0] += 1
        copy = push(full.at[rows, :], full.at[rows, :], send.at[k], recv.at[k], along(axis, y, x, d))
        sent.append(copy)
        return copy

    kinds = (0, 1)
    right, left, up, down = {}, {}, {}, {}
    fr, fl, fu, fd = {}, {}, {}, {}

    def spread(kind, a):
        up[kind, a] = put(kind, a, 0, 0, False, 1)
        down[kind, a] = put(kind, a, 0, 0, False, -1)

    def relay(kind, a):
        up[kind, a].wait_recv()
        fu[kind, a] = put(kind, a, -1, 1, False, 1)
        down[kind, a].wait_recv()
        fd[kind, a] = put(kind, a, 1, 2, False, -1)

    for kind in kinds:
        right[kind] = put(kind, 0, 0, 0, True, 1)
        left[kind] = put(kind, 0, 0, 0, True, -1)
    for kind in kinds:
        spread(kind, 0)
    early()
    for kind in kinds:
        right[kind].wait_recv()
        fr[kind] = put(kind, -1, 0, 1, True, 1)
        left[kind].wait_recv()
        fl[kind] = put(kind, 1, 0, 2, True, -1)
    for kind in kinds:
        spread(kind, -1)
        spread(kind, 1)
    for kind in kinds:
        relay(kind, 0)
    late()
    for kind in kinds:
        fr[kind].wait_recv()
        fl[kind].wait_recv()
        spread(kind, 2)
    for a in (-1, 1, 2):
        for kind in kinds:
            relay(kind, a)
    for a in (0, -1, 1, 2):
        for kind in kinds:
            fu[kind, a].wait_recv()
            fd[kind, a].wait_recv()
    return sent


def silu(v):
    return v * lax.logistic(v)


def silu_slope(v):
    s = lax.logistic(v)
    return s * (1.0 + v * (1.0 - s))


def whole_kernel(names, *refs):
    v = types.SimpleNamespace(**dict(zip(names, refs)))
    z, c, y, x = places()
    sample = y * 4 + x
    strip = z * 2 + c
    mate = other_core(c)
    mine = pl.multiple_of(c * BLOCK, 16)
    lane = pl.multiple_of(c * HALF, HALF)
    other_lane = pl.multiple_of((1 - c) * HALF, HALF)
    column = spot_column((SPOTS, HALF))
    inside = column < COLS
    zero = jnp.zeros((SPOTS, HALF), F32)

    def swap(src, dst, k):
        return push(src, dst, v.core_send.at[k], v.core_recv.at[k], mate)

    full, spots, proj = v.full, v.spots, v.proj
    shard = pl.ds(pl.multiple_of(sample * SHARD, SHARD), SHARD)
    loads = [pltpu.make_async_copy(v.w_point.at[:, pl.ds(lane, HALF)], full.at[shard, pl.ds(0, HALF)], v.local.at[0])]
    for t in range(9):
        loads.append(
            pltpu.make_async_copy(
                v.w_atrous.at[:, pl.ds(pl.multiple_of(t * FEAT + lane, HALF), HALF)],
                full.at[shard, pl.ds((t + 1) * HALF, HALF)],
                v.local.at[t + 1],
            )
        )
    loads.append(
        pltpu.make_async_copy(v.w_image.at[:, pl.ds(lane, HALF)], full.at[shard, pl.ds(WIDE, HALF)], v.local.at[10])
    )
    own_rows = pl.ds(pl.multiple_of(sample * 48, 16), 48)
    loads.append(pltpu.make_async_copy(v.w_proj, proj.at[own_rows, :], v.local.at[11]))
    inputs = [
        pltpu.make_async_copy(v.images, v.stage, v.local.at[12]),
        pltpu.make_async_copy(v.cotangent, v.cot_stage, v.local.at[13]),
    ]
    for load in loads + inputs:
        load.start()
    spots[pl.ds(mine, BLOCK), :] = jnp.zeros((BLOCK, CHANS), BF16)
    v.cot[pl.ds(mine, BLOCK), :] = jnp.zeros((BLOCK, HALF), BF16)
    v.cot_send[...] = jnp.zeros_like(v.cot_send)
    greet([strip_peer(strip, k) for k in range(1, 16)] + [sample_peer(sample, k) for k in range(1, 16)])
    for load in loads:
        load.wait()

    later = []

    def early():
        for load in inputs:
            load.wait()
        for r in range(ROWS):
            spots[pl.ds(pl.multiple_of(mine + r * PITCH, 16), COLS), :] = v.stage[r]
        later.append(swap(spots.at[pl.ds(mine, BLOCK), :], spots.at[pl.ds(mine, BLOCK), :], 0))
        for r in range(ROWS):
            v.cot_send[pl.ds(r * PITCH, COLS), :] = v.cot_stage[r, :, pl.ds(other_lane, HALF)]
            v.cot[pl.ds(pl.multiple_of(mine + r * PITCH, 16), COLS), :] = v.cot_stage[r, :, pl.ds(lane, HALF)]
        later.append(swap(v.cot_send, v.cot.at[pl.ds(mine, BLOCK), :], 1))
        later.extend(
            push(
                proj.at[own_rows, :], proj.at[own_rows, :], v.proj_send.at[k - 1], v.proj_recv.at[k - 1],
                sample_peer(sample, k),
            )
            for k in range(1, 16)
        )

    pools = []

    def late():
        later[0].wait_recv()

        def add_rows(i, total):
            return total + spots[pl.ds(pl.multiple_of(i * 16, 16), 16), :].astype(F32)

        sums = lax.fori_loop(0, SPOTS // 16, add_rows, jnp.zeros((16, CHANS), F32))
        v.pool_src[...] = jnp.sum(sums, axis=0, keepdims=True)
        pools.extend(
            push(v.pool_src, v.pool_slots.at[z], v.pool_send.at[k - 1], v.pool_recv.at[k - 1], z_peer(z, k))
            for k in range(1, 8)
        )
        v.pool_slots[z] = v.pool_src[...]

    ring_sent = ring_gather(full, y, x, v.gather_send, v.gather_recv, early, late)

    def multiply(n, carry):
        product = jnp.dot(
            spots[...], full[:, pl.ds(pl.multiple_of(n * FEAT, FEAT), FEAT)], preferred_element_type=F32
        )
        v.taps[2 * n] = product[:, :HALF]
        v.taps[2 * n + 1] = product[:, HALF:]
        return carry

    lax.fori_loop(0, TAPS // 2, multiply, 0)

    def row_tap(r):
        first = 1 + 3 * (r + 1)
        return v.taps[first + 1] + moved(v.taps[first], -RATE, column) + moved(v.taps[first + 2], RATE, column)

    v.outer[0] = row_tap(-1).astype(BF16)
    below = push(v.outer.at[0], v.halo.at[0], v.halo_send.at[0], v.halo_recv.at[0], z_peer(z, 2))
    v.outer[1] = row_tap(1).astype(BF16)
    above = push(v.outer.at[1], v.halo.at[1], v.halo_send.at[1], v.halo_recv.at[1], z_peer(z, -2))
    v.centre[...] = row_tap(0)
    for copy in pools:
        copy.wait()
    pooled = (jnp.sum(v.pool_slots[...], axis=0) / SAMPLE_AREA).astype(BF16)
    image = jnp.dot(
        jnp.broadcast_to(pooled, (16, CHANS)), full[:, pl.ds(WIDE, HALF)], preferred_element_type=F32
    )
    v.images_half[c] = image[0:8]
    later.append(swap(v.images_half.at[c], v.images_half.at[c], 2))

    def to_samples(src_of, slots, send, recv):
        return [
            push(
                src_of(lax.rem(sample + k, 16)), slots.at[sample], send.at[k - 1], recv.at[k - 1],
                sample_peer(sample, k),
            )
            for k in range(1, 16)
        ]

    for k in range(16):
        v.pool_rows[k] = jnp.broadcast_to(pooled[:, k * SHARD : (k + 1) * SHARD].astype(F32), (8, SHARD))

    def totals(i, rows, meanwhile):
        for k, row in enumerate(rows):
            v.ar_src[i, pl.ds(k, 1), :] = row
        copies = [
            push(v.ar_src.at[i], v.ar_z.at[i, z], v.z_send.at[i, k - 1], v.z_recv.at[i, k - 1], z_peer(z, k))
            for k in range(1, 8)
        ]
        v.ar_z[i, z] = v.ar_src[i]
        meanwhile[0]()
        for copy in copies:
            copy.wait()
        whole = jnp.sum(v.ar_z[i], axis=0)
        v.ar_mid[i] = whole
        copies = [
            push(
                v.ar_mid.at[i], v.ar_xy.at[i, sample], v.xy_send.at[i, k - 1], v.xy_recv.at[i, k - 1],
                sample_peer(sample, k),
            )
            for k in range(1, 16)
        ]
        v.ar_xy[i, sample] = whole
        meanwhile[1]()
        for copy in copies:
            copy.wait()
        total = jnp.sum(v.ar_xy[i], axis=0)
        return [whole[k : k + 1] for k in range(4)], [total[k : k + 1] for k in range(4)]

    def down(a):
        return jnp.sum(a, axis=0, keepdims=True)

    def finish(total, power):
        centre = total / TOTAL_AREA
        return centre, lax.rsqrt(power / TOTAL_AREA - centre * centre + EPSILON)

    def mean_of(both):
        return (jnp.sum(both[0]) + jnp.sum(both[1])) * (1.0 / FEAT)

    nothing = lambda: None
    below.wait()
    above.wait()
    point = v.taps[0]
    atrous = (
        v.centre[...]
        + jnp.where(z >= 2, v.halo[0].astype(F32), zero)
        + jnp.where(z < 6, v.halo[1].astype(F32), zero)
    )
    v.centre[...] = atrous
    keep = types.SimpleNamespace()

    def send_pools():
        keep.pools = to_samples(lambda j: v.pool_rows.at[j], v.pool_all, v.pall_send, v.pall_recv)
        v.pool_all[sample] = v.pool_rows[sample]

    def image_forward():
        later[-1].wait_recv()
        halves = [v.images_half[0][0:1], v.images_half[1][0:1]]
        image_mean = mean_of(halves)
        apart = [h - image_mean for h in halves]
        keep.layer_scale = lax.rsqrt(jnp.full((1, HALF), mean_of([a * a for a in apart]) + EPSILON, F32))
        keep.layer_norm = [a * keep.layer_scale for a in apart]
        keep.relu_image = jnp.concatenate([silu(a) for a in keep.layer_norm], axis=1).astype(BF16)
        for copy in later[2:17]:
            copy.wait_recv()
        keep.image_row = jnp.dot(
            jnp.broadcast_to(keep.relu_image, (16, FEAT)),
            proj[pl.ds(2 * FEAT, FEAT), pl.ds(lane, HALF)],
            preferred_element_type=F32,
        )[0:1]

    _, (s0, s1, s2, s3) = totals(
        0, [down(point), down(point * point), down(atrous), down(atrous * atrous)], (send_pools, image_forward)
    )
    centre_p, scale_p = finish(s0, s1)
    centre_a, scale_a = finish(s2, s3)
    v.norm_p[...] = (point - centre_p) * scale_p
    v.norm_a[...] = (v.centre[...] - centre_a) * scale_a
    relu = v.relu
    relu[c, :, pl.ds(0, HALF)] = jnp.where(inside, silu(v.norm_p[...]), 0.0).astype(BF16)
    relu[c, :, pl.ds(HALF, HALF)] = jnp.where(inside, silu(v.norm_a[...]), 0.0).astype(BF16)
    swap_relu = swap(relu.at[c], relu.at[c], 3)

    def mix_term(k):
        total = None
        for b in range(2):
            first = pl.multiple_of(k * HALF + b * FEAT, HALF)
            term = jnp.dot(
                relu[k, :, pl.ds(b * HALF, HALF)],
                proj[pl.ds(first, HALF), pl.ds(lane, HALF)],
                preferred_element_type=F32,
            )
            total = term if total is None else total + term
        return total

    mixed = mix_term(c) + keep.image_row
    swap_relu.wait()
    mixed = jnp.where(inside, mixed + mix_term(1 - c), 0.0)
    v.mixed[...] = mixed

    def slope_point():
        v.slope_p[...] = silu_slope(v.norm_p[...])

    def slope_atrous():
        v.slope_a[...] = silu_slope(v.norm_a[...])

    blank = jnp.zeros((1, HALF), F32)
    (mixed_sample, _, _, _), (s0, s1, _, _) = totals(
        1, [down(mixed), down(mixed * mixed), blank, blank], (slope_point, slope_atrous)
    )
    centre_m, scale_m = finish(s0, s1)
    norm_mix = (v.mixed[...] - centre_m) * scale_m
    v.mixed[...] = norm_mix
    later[1].wait_recv()
    sigma = lax.logistic(norm_mix)
    upstream = jnp.where(inside, v.cot[...].astype(F32) * (sigma * (1.0 + norm_mix * (1.0 - sigma))), 0.0)
    v.upstream[...] = upstream

    def make_result():
        result = silu(v.mixed[...]).astype(BF16)
        v.result_send[0] = result[:BLOCK]
        v.result_send[1] = result[BLOCK:]
        keep.result = swap(v.result_send.at[1 - c], v.result_half, 4)

    def store_result():
        keep.result.wait_recv()
        for r in range(ROWS):
            rows = pl.ds(r * PITCH, COLS)
            v.out_result[r, :, pl.ds(lane, HALF)] = v.result_send[c, rows, :]
            v.out_result[r, :, pl.ds(other_lane, HALF)] = v.result_half[rows, :]

    (up_sample, _, _, _), (s0, s1, _, _) = totals(
        2, [down(upstream), down(upstream * norm_mix), blank, blank], (make_result, store_result)
    )
    mean_u = s0 / TOTAL_AREA
    mean_un = s1 / TOTAL_AREA
    grad_mix = jnp.where(inside, (v.upstream[...] - mean_u - v.mixed[...] * mean_un) * scale_m, 0.0)
    mix, columns = v.mix, v.columns
    mix[c] = grad_mix.astype(BF16)
    swap_mix = swap(mix.at[c], mix.at[c], 5)
    norm_sample = (mixed_sample - SAMPLE_AREA * centre_m) * scale_m
    column_total = (up_sample - SAMPLE_AREA * mean_u - mean_un * norm_sample) * scale_m
    columns[c] = jnp.broadcast_to(column_total, (8, HALF))
    swap_columns = swap(columns.at[c], columns.at[c], 6)

    def back_term(first, k):
        return lax.dot_general(
            mix[k],
            proj[pl.ds(pl.multiple_of(first + lane, HALF), HALF), pl.ds(pl.multiple_of(k * HALF, HALF), HALF)],
            (((1,), (1,)), ((), ())),
            preferred_element_type=F32,
        )

    back_p = back_term(0, c)
    back_a = back_term(FEAT, c)
    swap_mix.wait()
    up_point = (back_p + back_term(0, 1 - c)) * v.slope_p[...]
    up_atrous = (back_a + back_term(FEAT, 1 - c)) * v.slope_a[...]
    v.slope_p[...] = up_point
    v.slope_a[...] = up_atrous

    def image_backward():
        swap_columns.wait()
        column_b = jnp.concatenate([columns[0][0:1], columns[1][0:1]], axis=1).astype(BF16)
        back_image = lax.dot_general(
            jnp.broadcast_to(column_b, (16, FEAT)),
            proj[pl.ds(2 * FEAT, FEAT), :],
            (((1,), (1,)), ((), ())),
            preferred_element_type=F32,
        )
        layer_norm = keep.layer_norm
        up_image = [back_image[0:1, k * HALF : (k + 1) * HALF] * silu_slope(layer_norm[k]) for k in range(2)]
        mean_up = mean_of(up_image)
        mean_up_norm = mean_of([up_image[k] * layer_norm[k] for k in range(2)])
        image_grad = jnp.concatenate(
            [(up_image[k] - mean_up - layer_norm[k] * mean_up_norm) * keep.layer_scale for k in range(2)], axis=1
        )
        v.image_grad[...] = jnp.broadcast_to(image_grad.astype(BF16).astype(F32), (8, FEAT))
        keep.images = to_samples(lambda j: v.image_grad, v.image_all, v.image_send, v.image_recv)
        v.image_all[sample] = v.image_grad[...]

    def proj_gradient():
        for k in range(2):
            part = lax.dot_general(
                relu[k], mix[c], (((0,), (0,)), ((), ())), preferred_element_type=F32
            ) * FACTOR
            v.proj_part[pl.ds(k * HALF, HALF), :] = part[:HALF].astype(BF16)
            v.proj_part[pl.ds(FEAT + k * HALF, HALF), :] = part[HALF:].astype(BF16)
        once = lax.broadcasted_iota(jnp.int32, (16, FEAT), 0) == 0
        gate = jnp.where(z == 0, FACTOR, 0.0).astype(F32)
        outer = lax.dot_general(
            jnp.where(once, jnp.broadcast_to(keep.relu_image.astype(F32), (16, FEAT)), 0.0).astype(BF16),
            jnp.broadcast_to(columns[c][0:1], (16, HALF)).astype(BF16),
            (((0,), (0,)), ((), ())),
            preferred_element_type=F32,
        )
        v.proj_part[pl.ds(2 * FEAT, FEAT), :] = (outer * gate).astype(BF16)

    _, (s0, s1, s2, s3) = totals(
        3,
        [down(up_point), down(up_point * v.norm_p[...]), down(up_atrous), down(up_atrous * v.norm_a[...])],
        (image_backward, proj_gradient),
    )

    def back_norm(up, norm, first, second, scale):
        grad = (up - first / TOTAL_AREA - norm * (second / TOTAL_AREA)) * scale
        return jnp.where(inside, grad, 0.0)

    grad_atrous = back_norm(v.slope_a[...], v.norm_a[...], s2, s3, scale_a)
    v.grad_atrous[...] = grad_atrous.astype(BF16)
    upper = push(v.grad_atrous, v.back_halo.at[1], v.halo_send.at[2], v.halo_recv.at[2], z_peer(z, 2))
    lower = push(v.grad_atrous, v.back_halo.at[0], v.halo_send.at[3], v.halo_recv.at[3], z_peer(z, -2))
    proj_copies = [
        push(
            v.proj_part.at[pl.ds(pl.multiple_of(lax.rem(sample + k, 16) * 48, 16), 48), :], v.proj_slots.at[sample],
            v.pgrad_send.at[k - 1], v.pgrad_recv.at[k - 1], sample_peer(sample, k),
        )
        for k in range(1, 16)
    ]
    v.proj_slots[sample] = v.proj_part[own_rows, :]
    cols = v.cols
    cols[:, pl.ds(0, HALF)] = back_norm(v.slope_p[...], v.norm_p[...], s0, s1, scale_p).astype(BF16)

    def fill(r, source):
        for s in (-1, 0, 1):
            t = 1 + 3 * (r + 1) + (s + 1)
            cols[:, pl.ds(t * HALF, HALF)] = moved(source, -RATE * s, column).astype(BF16)

    fill(0, v.grad_atrous[...].astype(F32))
    upper.wait()
    fill(1, jnp.where(z >= 2, v.back_halo[1].astype(F32), zero))
    lower.wait()
    fill(-1, jnp.where(z < 6, v.back_halo[0].astype(F32), zero))

    partial, opposite, beside = v.partial, v.opposite, v.beside

    def weight_block(dy):
        base = lax.rem(y + dy + 4, 4) * 512

        def weight_part(k, carry):
            at = pl.ds(pl.multiple_of(base + k * FEAT, FEAT), FEAT)
            part = lax.dot_general(
                spots[:, at], cols[...], (((0,), (0,)), ((), ())), preferred_element_type=F32
            )
            partial[at, :] = (part * FACTOR).astype(BF16)
            return carry

        lax.fori_loop(0, 2, weight_part, 0)

    count = [0]
    done = []

    class Ring:
        def __init__(self, slot, axis, base, index):
            self.slot, self.axis, self.base, self.index = slot, axis, base, index

        def rows(self, o, start, size):
            return pl.ds(pl.multiple_of(self.index(o) * SHARD + self.base + start, 32), size)

        def put(self, src, dst, d):
            k = count[0]
            count[0] += 1
            copy = push(src, dst, v.ring_send.at[k], v.ring_recv.at[k], along(self.axis, y, x, d))
            done.append(copy)
            return copy

        def far(self):
            s = self.slot
            self.m0 = self.put(partial.at[self.rows(2, 0, 32), :], opposite.at[s, 0], 1)
            self.m1 = self.put(partial.at[self.rows(2, 32, 32), :], opposite.at[s, 1], -1)

        def near_up(self):
            self.m2 = self.put(partial.at[self.rows(1, 32, 32), :], beside.at[self.slot, 0, pl.ds(32, 32), :], 1)

        def near_down(self):
            self.m3 = self.put(partial.at[self.rows(-1, 0, 32), :], beside.at[self.slot, 1, pl.ds(0, 32), :], -1)

        def relay(self):
            s = self.slot
            self.m0.wait_recv()
            at = self.rows(1, 0, 32)
            partial[at, :] = (partial[at, :].astype(F32) + opposite[s, 0].astype(F32)).astype(BF16)
            self.m4 = self.put(partial.at[at, :], beside.at[s, 0, pl.ds(0, 32), :], 1)
            self.m1.wait_recv()
            at = self.rows(-1, 32, 32)
            partial[at, :] = (partial[at, :].astype(F32) + opposite[s, 1].astype(F32)).astype(BF16)
            self.m5 = self.put(partial.at[at, :], beside.at[s, 1, pl.ds(32, 32), :], -1)

        def close(self):
            s = self.slot
            for m in (self.m2, self.m3, self.m4, self.m5):
                m.wait_recv()
            at = self.rows(0, 0, 64)
            partial[at, :] = (
                partial[at, :].astype(F32) + beside[s, 0].astype(F32) + beside[s, 1].astype(F32)
            ).astype(BF16)

    def block(dy, dx):
        return lax.rem(y + dy + 4, 4) * 4 + lax.rem(x + dx + 4, 4)

    order = (2, 1, -1, 0)
    by_y = [Ring(n, "y", 0, functools.partial(lambda a, o: block(o, a), a)) for n, a in enumerate(order)]
    by_x = [Ring(4 + n, "x", 64, functools.partial(lambda a, o: block(a, o), a)) for n, a in enumerate(order)]
    last = [
        Ring(8, "x", 0, lambda o: block(0, o)),
        Ring(9, "y", 64, lambda o: block(o, 0)),
    ]
    for n, dy in enumerate(order):
        weight_block(dy)
        by_x[n].far()
        if dy == 2:
            for ring in by_y:
                ring.far()
        if dy == 1:
            for ring in by_y:
                ring.near_up()
        if dy == -1:
            for ring in by_y:
                ring.near_down()
        by_x[n].near_up()
        by_x[n].near_down()

    half_grad = v.image_grad[:, pl.ds(lane, HALF)]
    grad_rows = jnp.concatenate([half_grad, half_grad], axis=0).astype(BF16)

    def input_part(k, carry):
        at = pl.ds(pl.multiple_of(k * FEAT, FEAT), FEAT)
        part = lax.dot_general(
            cols[...], full[at, pl.ds(0, WIDE)], (((1,), (1,)), ((), ())), preferred_element_type=F32
        )
        pool = lax.dot_general(
            grad_rows, full[at, pl.ds(WIDE, HALF)], (((1,), (1,)), ((), ())), preferred_element_type=F32
        )[0:1] / SAMPLE_AREA
        part = part + pool
        v.pair[0] = part[:BLOCK]
        v.pair[1] = part[BLOCK:]
        v.own[k] = v.pair[c]
        v.away[k] = v.pair[1 - c].astype(BF16)
        return carry

    lax.fori_loop(0, 4, input_part, 0)
    for n in range(4):
        by_x[n].relay()
        by_y[n].relay()
    lax.fori_loop(4, 8, input_part, 0)
    swap_input = swap(v.away, v.came, 7)
    for n in range(4):
        by_y[n].close()
        by_x[n].close()
        if n == 0:
            for ring in last:
                ring.far()
        if n == 1:
            for ring in last:
                ring.near_up()
        if n == 2:
            for ring in last:
                ring.near_down()
    for ring in last:
        ring.relay()

    for copy in proj_copies:
        copy.wait()
    v.proj_sum[...] = jnp.sum(v.proj_slots[...].astype(F32), axis=0).astype(BF16)

    def to_strips(src, dst, send, recv):
        return [push(src, dst, send.at[k - 1], recv.at[k - 1], strip_peer(strip, k)) for k in range(1, 16)]

    spread = to_strips(v.proj_sum, v.proj_all.at[strip], v.spread_send, v.spread_recv)
    v.proj_all[strip] = v.proj_sum[...]

    for ring in last:
        ring.close()
    here = sample * SHARD
    z_copies = [
        push(
            partial.at[pl.ds(pl.multiple_of(here + lax.rem(z + k, 8) * 16, 16), 16), :],
            v.z_slots.at[z], v.zsum_send.at[k - 1], v.zsum_recv.at[k - 1], z_peer(z, k),
        )
        for k in range(1, 8)
    ]
    v.z_slots[z] = partial[pl.ds(pl.multiple_of(here + z * 16, 16), 16), :]

    swap_input.wait()
    for k in range(CHANS // FEAT):
        total = (v.own[k] + v.came[k].astype(F32)).astype(BF16)
        for r in range(ROWS):
            v.out_input[r, :, pl.ds(k * FEAT, FEAT)] = total[r * PITCH : r * PITCH + COLS]

    for copy in z_copies:
        copy.wait()
    v.z_sum[...] = jnp.sum(v.z_slots[...].astype(F32), axis=0).astype(BF16)
    my_rows = pl.ds(pl.multiple_of(z * 16, 16), 16)
    joined = v.joined
    all_copies = to_strips(v.z_sum, joined.at[c, my_rows, :], v.all_send, v.all_recv)
    joined[c, my_rows, :] = v.z_sum[...]

    for copy in keep.pools + keep.images:
        copy.wait()
    v.out_image[...] = (
        lax.dot_general(
            v.pool_all[...][:, 0, :].astype(BF16), v.image_all[...][:, 0, :].astype(BF16),
            (((0,), (0,)), ((), ())), preferred_element_type=F32,
        )
        * FACTOR
    )
    for copy in spread:
        copy.wait()
    for k in range(2):
        total = v.proj_all[k].astype(F32)
        for level in range(1, 8):
            total = total + v.proj_all[2 * level + k].astype(F32)
        v.out_proj[:, pl.ds(k * HALF, HALF)] = total
    for copy in ring_sent + later + done:
        copy.wait_send()
    keep.result.wait_send()
    for copy in all_copies:
        copy.wait()
    for k in range(2):
        v.out_point[:, pl.ds(k * HALF, HALF)] = joined[k, :, pl.ds(0, HALF)].astype(F32)
        for t in range(9):
            v.out_atrous[:, pl.ds(t * FEAT + k * HALF, HALF)] = joined[k, :, pl.ds((t + 1) * HALF, HALF)].astype(F32)


VMEM = pl.BlockSpec(memory_space=pltpu.VMEM)
ANY = pl.BlockSpec(memory_space=pl.ANY)


def dma(*shape):
    return pltpu.SemaphoreType.DMA(shape)


def sized(dtype, *shape):
    return jax.ShapeDtypeStruct(shape, dtype)


ARGS = ("images", "w_point", "w_atrous", "w_image", "w_proj", "cotangent")
OUTS = (
    ("out_result", sized(BF16, ROWS, COLS, FEAT)),
    ("out_input", sized(BF16, ROWS, COLS, CHANS)),
    ("out_point", sized(F32, SHARD, FEAT)),
    ("out_atrous", sized(F32, SHARD, 9 * FEAT)),
    ("out_image", sized(F32, SHARD, FEAT)),
    ("out_proj", sized(F32, 48, FEAT)),
)
SCRATCH = (
    ("stage", (ROWS, COLS, CHANS), BF16),
    ("cot_stage", (ROWS, COLS, FEAT), BF16),
    ("spots", (SPOTS, CHANS), BF16),
    ("full", (CHANS, WIDER), BF16),
    ("proj", (3 * FEAT, FEAT), BF16),
    ("taps", (TAPS, SPOTS, HALF), F32),
    ("pool_src", (1, CHANS), F32),
    ("pool_slots", (8, 1, CHANS), F32),
    ("pool_rows", (16, 8, SHARD), F32),
    ("pool_all", (16, 8, SHARD), F32),
    ("image_grad", (8, FEAT), F32),
    ("image_all", (16, 8, FEAT), F32),
    ("images_half", (2, 8, HALF), F32),
    ("outer", (2, SPOTS, HALF), BF16),
    ("halo", (2, SPOTS, HALF), BF16),
    ("centre", (SPOTS, HALF), F32),
    ("norm_p", (SPOTS, HALF), F32),
    ("norm_a", (SPOTS, HALF), F32),
    ("slope_p", (SPOTS, HALF), F32),
    ("slope_a", (SPOTS, HALF), F32),
    ("mixed", (SPOTS, HALF), F32),
    ("upstream", (SPOTS, HALF), F32),
    ("relu", (2, SPOTS, FEAT), BF16),
    ("mix", (2, SPOTS, HALF), BF16),
    ("columns", (2, 8, HALF), F32),
    ("cot", (SPOTS, HALF), BF16),
    ("cot_send", (BLOCK, HALF), BF16),
    ("result_send", (2, BLOCK, HALF), BF16),
    ("result_half", (BLOCK, HALF), BF16),
    ("ar_src", (4, 4, HALF), F32),
    ("ar_mid", (4, 4, HALF), F32),
    ("ar_z", (4, 8, 4, HALF), F32),
    ("ar_xy", (4, 16, 4, HALF), F32),
    ("proj_part", (3 * FEAT, HALF), BF16),
    ("proj_slots", (16, 48, HALF), BF16),
    ("proj_sum", (48, HALF), BF16),
    ("proj_all", (16, 48, HALF), BF16),
    ("grad_atrous", (SPOTS, HALF), BF16),
    ("back_halo", (2, SPOTS, HALF), BF16),
    ("cols", (SPOTS, WIDE), BF16),
    ("partial", (CHANS, WIDE), BF16),
    ("opposite", (10, 2, 32, WIDE), BF16),
    ("beside", (10, 2, 64, WIDE), BF16),
    ("pair", (2, BLOCK, FEAT), F32),
    ("own", (8, BLOCK, FEAT), F32),
    ("away", (8, BLOCK, FEAT), BF16),
    ("came", (8, BLOCK, FEAT), BF16),
    ("z_slots", (8, 16, WIDE), BF16),
    ("z_sum", (16, WIDE), BF16),
    ("joined", (2, SHARD, WIDE), BF16),
)
SEMAPHORES = (
    ("local", (14,)),
    ("core", (8,)),
    ("gather", (40,)),
    ("proj", (15,)),
    ("pool", (7,)),
    ("pall", (15,)),
    ("image", (15,)),
    ("halo", (4,)),
    ("z", (4, 7)),
    ("xy", (4, 15)),
    ("pgrad", (15,)),
    ("ring", (60,)),
    ("zsum", (7,)),
    ("spread", (15,)),
    ("all", (15,)),
)


def on_device(images, w_point, w_atrous, w_image, w_proj, cotangent):
    names = list(ARGS) + [n for n, _ in OUTS] + [n for n, _, _ in SCRATCH]
    scratch = [pltpu.VMEM(shape, dtype) for _, shape, dtype in SCRATCH]
    for name, shape in SEMAPHORES:
        kinds = ("local",) if name == "local" else (name + "_send", name + "_recv")
        for kind in kinds:
            names.append(kind)
            scratch.append(dma(*shape))
    outs = pl.pallas_call(
        functools.partial(whole_kernel, tuple(names)),
        out_shape=[shape for _, shape in OUTS],
        in_specs=[ANY] * 6,
        out_specs=[VMEM] * 6,
        scratch_shapes=scratch,
        compiler_params=pltpu.CompilerParams(
            collective_id=0, has_side_effects=True, vmem_limit_bytes=60 << 20
        ),
        name="whole",
    )(images[0], w_point, w_atrous, w_image, w_proj, cotangent[0])
    return (outs[0][None], outs[1][None], *outs[2:])


def solution(mesh):
    finer = Mesh(mesh.devices.reshape(8, 2, 4, 4), STRIP + SAMPLE)
    placed = (
        P(SAMPLE, STRIP, None, None),
        P(SAMPLE, None),
        P(SAMPLE, None),
        P(SAMPLE, None),
        P(SAMPLE, None),
        P(SAMPLE, STRIP, None, None),
    )
    return jax.shard_map(
        on_device,
        mesh=finer,
        in_specs=placed,
        out_specs=(
            P(SAMPLE, STRIP, None, None),
            P(SAMPLE, STRIP, None, None),
            P(SAMPLE, None),
            P(SAMPLE, None),
            P(SAMPLE, None),
            P(SAMPLE, None),
        ),
        check_vma=False,
    )
```

time: 209 us -> 184 us (0.88)
  Pallas kernels: 195 us -> 176 us
  local copies, waits for them, and re-layouts: 13.7 us -> 7.23 us
    pallas_call x3 -> x1, Pallas kernels: 195 us -> 176 us  [on_device(): pl.pallas_call(functools.partial(whole_kernel, tuple(names)), out_shape=[...]
    unnamed x36 -> x14, local copies, waits for them, and re-layouts: 13.7 us -> 7.23 us
where the time goes in v3:
time: 184 us
  Pallas kernels  176 us (96%)
  local copies, waits for them, and re-layouts  7.23 us (4%)
    pallas_call x1, Pallas kernels, on_device(): pl.pallas_call(functools.partial(whole_kernel, tuple(names)), out_shape=[...  176 us
    unnamed x14, local copies, waits for them, and re-layouts  7.23 us

profile of v3, /device:TPU:1, one launch (start us, length us, event | category | flops | bytes accessed | tf_op | source)
XLA Modules:
  0.0 183.8 jit_solution(7754386989028884590)
XLA Ops:
  0.6 175.9 %whole.1 = (bf16[3,108,256]{2,1,0:T(8,128)(2,1)}, bf16[3,108,2048]{2,1,0:T(8,128)(2,1)}, f32[128,256]{1,0:T(8,128)}, f32[128,2304]{1,0:T(8,128)}, f32[128,256]{1,0:T(8,128)}, /*index=5*/f32[48,256]{1,0:T(8,128)}) custom-call(bf16[3,108,2048]{2,1,0:T(8,128)(2,1)} %bitcast.5, bf16[128,256]{1,0:T(8,128)(2,1)} %refs_1_.1, bf16[128,2304]{1,0:T(8,128)(2,1)} %refs_2_.1, ...), custom_call_target="tpu_custom_call" | custom-call | tf_op jit(solution)/shard_map/whole/pallas_call | solution.py:818
  176.5 1.6 copy.18
  178.1 0.0 copy-start.2
  178.1 0.0 copy-start
  178.1 2.7 %copy.19 = bf16[1,3,108,2048]{3,2,1,0:T(8,128)(2,1)} copy(bf16[1,3,108,2048]{3,2,1,0:T(8,128)(2,1)} %bitcast.4) | data formatting | bytes 2654208
  180.8 0.0 copy-done.2
  180.8 0.0 copy-start.1
  180.8 0.7 copy.20
  181.5 0.0 copy-done
  181.5 0.0 copy-start.3
  181.5 1.0 copy.21
  182.5 0.0 copy-done.1
  182.5 0.7 copy.22
  183.1 0.0 copy-done.3
  183.1 0.6 copy.23
Async XLA Ops:
  178.1 2.7 %copy-start.2 = (f32[128,256]{1,0:T(8,128)S(1)}, f32[128,256]{1,0:T(8,128)}, u32[]{:S(2)}) copy-start(f32[128,256]{1,0:T(8,128)} %get-tuple-element.26) | copy-start | bytes 393220
  178.1 3.3 %copy-start = (f32[128,2304]{1,0:T(8,128)S(1)}, f32[128,2304]{1,0:T(8,128)}, u32[]{:S(2)}) copy-start(f32[128,2304]{1,0:T(8,128)} %get-tuple-element.27) | copy-start | bytes 3538948
  180.8 1.7 copy-start.1
  181.5 1.7 copy-start.3

commit v4 on v3

--- a/solution.py
+++ b/solution.py
@@ -25,6 +25,7 @@
 PITCH = 112
 BLOCK = ROWS * PITCH
 SPOTS = 2 * BLOCK
+DEPTH = 768
 TAPS = 10
 WIDE = TAPS * HALF
 WIDER = WIDE + HALF
@@ -57,15 +58,11 @@
     return {"sample_0": lax.div(other, 4), "sample_1": lax.rem(other, 4)}
 
 
-def strip_peer(me, k):
-    other = lax.rem(me + k, 16)
-    return {"strip_0": lax.div(other, 2), "strip_1": lax.rem(other, 2)}
-
-
-def greet(peers):
+def greet(peers, meanwhile):
     barrier = pltpu.get_barrier_semaphore()
     for peer in peers:
         pl.semaphore_signal(barrier, inc=1, device_id=peer, device_id_type=MESH_ID)
+    meanwhile()
     pl.semaphore_wait(barrier, len(peers))
 
 
@@ -174,7 +171,6 @@
     v = types.SimpleNamespace(**dict(zip(names, refs)))
     z, c, y, x = places()
     sample = y * 4 + x
-    strip = z * 2 + c
     mate = other_core(c)
     mine = pl.multiple_of(c * BLOCK, 16)
     lane = pl.multiple_of(c * HALF, HALF)
@@ -201,17 +197,25 @@
         pltpu.make_async_copy(v.w_image.at[:, pl.ds(lane, HALF)], full.at[shard, pl.ds(WIDE, HALF)], v.local.at[10])
     )
     own_rows = pl.ds(pl.multiple_of(sample * 48, 16), 48)
-    loads.append(pltpu.make_async_copy(v.w_proj, proj.at[own_rows, :], v.local.at[11]))
+    half_lanes = pl.ds(lane, HALF)
+    loads.append(
+        pltpu.make_async_copy(v.w_proj.at[:, half_lanes], proj.at[own_rows, half_lanes], v.local.at[11])
+    )
     inputs = [
         pltpu.make_async_copy(v.images, v.stage, v.local.at[12]),
         pltpu.make_async_copy(v.cotangent, v.cot_stage, v.local.at[13]),
     ]
     for load in loads + inputs:
         load.start()
-    spots[pl.ds(mine, BLOCK), :] = jnp.zeros((BLOCK, CHANS), BF16)
-    v.cot[pl.ds(mine, BLOCK), :] = jnp.zeros((BLOCK, HALF), BF16)
-    v.cot_send[...] = jnp.zeros_like(v.cot_send)
-    greet([strip_peer(strip, k) for k in range(1, 16)] + [sample_peer(sample, k) for k in range(1, 16)])
+
+    def clear():
+        spots[pl.ds(mine, BLOCK), :] = jnp.zeros((BLOCK, CHANS), BF16)
+        spots[pl.ds(SPOTS, DEPTH - SPOTS), :] = jnp.zeros((DEPTH - SPOTS, CHANS), BF16)
+        v.cols[pl.ds(SPOTS, DEPTH - SPOTS), :] = jnp.zeros((DEPTH - SPOTS, WIDE), BF16)
+        v.cot[pl.ds(mine, BLOCK), :] = jnp.zeros((BLOCK, HALF), BF16)
+        v.cot_send[...] = jnp.zeros_like(v.cot_send)
+
+    greet([mate] + [z_peer(z, k) for k in range(1, 8)] + [sample_peer(sample, k) for k in range(1, 16)], clear)
     for load in loads:
         load.wait()
 
@@ -227,13 +231,6 @@
             v.cot_send[pl.ds(r * PITCH, COLS), :] = v.cot_stage[r, :, pl.ds(other_lane, HALF)]
             v.cot[pl.ds(pl.multiple_of(mine + r * PITCH, 16), COLS), :] = v.cot_stage[r, :, pl.ds(lane, HALF)]
         later.append(swap(v.cot_send, v.cot.at[pl.ds(mine, BLOCK), :], 1))
-        later.extend(
-            push(
-                proj.at[own_rows, :], proj.at[own_rows, :], v.proj_send.at[k - 1], v.proj_recv.at[k - 1],
-                sample_peer(sample, k),
-            )
-            for k in range(1, 16)
-        )
 
     pools = []
 
@@ -251,11 +248,26 @@
         )
         v.pool_slots[z] = v.pool_src[...]
 
+        def flip(k, carry):
+            at = pl.ds(pl.multiple_of(k * SHARD, SHARD), SHARD)
+            v.flipped[at, :] = spots[:, at].T
+            return carry
+
+        lax.fori_loop(0, CHANS // SHARD, flip, 0)
+
     ring_sent = ring_gather(full, y, x, v.gather_send, v.gather_recv, early, late)
+
+    proj_copies = [
+        push(
+            proj.at[own_rows, half_lanes], proj.at[own_rows, half_lanes],
+            v.proj_send.at[k - 1], v.proj_recv.at[k - 1], sample_peer(sample, k),
+        )
+        for k in range(1, 16)
+    ]
 
     def multiply(n, carry):
         product = jnp.dot(
-            spots[...], full[:, pl.ds(pl.multiple_of(n * FEAT, FEAT), FEAT)], preferred_element_type=F32
+            spots[pl.ds(0, SPOTS), :], full[:, pl.ds(pl.multiple_of(n * FEAT, FEAT), FEAT)], preferred_element_type=F32
         )
         v.taps[2 * n] = product[:, :HALF]
         v.taps[2 * n + 1] = product[:, HALF:]
@@ -272,14 +284,7 @@
     v.outer[1] = row_tap(1).astype(BF16)
     above = push(v.outer.at[1], v.halo.at[1], v.halo_send.at[1], v.halo_recv.at[1], z_peer(z, -2))
     v.centre[...] = row_tap(0)
-    for copy in pools:
-        copy.wait()
-    pooled = (jnp.sum(v.pool_slots[...], axis=0) / SAMPLE_AREA).astype(BF16)
-    image = jnp.dot(
-        jnp.broadcast_to(pooled, (16, CHANS)), full[:, pl.ds(WIDE, HALF)], preferred_element_type=F32
-    )
-    v.images_half[c] = image[0:8]
-    later.append(swap(v.images_half.at[c], v.images_half.at[c], 2))
+    keep = types.SimpleNamespace()
 
     def to_samples(src_of, slots, send, recv):
         return [
@@ -290,8 +295,6 @@
             for k in range(1, 16)
         ]
 
-    for k in range(16):
-        v.pool_rows[k] = jnp.broadcast_to(pooled[:, k * SHARD : (k + 1) * SHARD].astype(F32), (8, SHARD))
 
     def totals(i, rows, meanwhile):
         for k, row in enumerate(rows):
@@ -340,22 +343,36 @@
         + jnp.where(z < 6, v.halo[1].astype(F32), zero)
     )
     v.centre[...] = atrous
-    keep = types.SimpleNamespace()
 
     def send_pools():
+        for k in range(16):
+            rows = keep.pooled[:, k * SHARD : (k + 1) * SHARD].astype(F32)
+            v.pool_rows[k] = jnp.broadcast_to(rows, (8, SHARD))
         keep.pools = to_samples(lambda j: v.pool_rows.at[j], v.pool_all, v.pall_send, v.pall_recv)
         v.pool_all[sample] = v.pool_rows[sample]
 
+    def image_product():
+        for copy in pools:
+            copy.wait()
+        keep.pooled = (jnp.sum(v.pool_slots[...], axis=0) / SAMPLE_AREA).astype(BF16)
+        image = jnp.dot(
+            jnp.broadcast_to(keep.pooled, (16, CHANS)), full[:, pl.ds(WIDE, HALF)], preferred_element_type=F32
+        )
+        v.images_half[c] = image[0:8]
+        later.append(swap(v.images_half.at[c], v.images_half.at[c], 2))
+        for copy in proj_copies:
+            copy.wait()
+        later.append(swap(proj.at[:, half_lanes], proj.at[:, half_lanes], 8))
+
     def image_forward():
-        later[-1].wait_recv()
+        later[-2].wait_recv()
         halves = [v.images_half[0][0:1], v.images_half[1][0:1]]
         image_mean = mean_of(halves)
         apart = [h - image_mean for h in halves]
         keep.layer_scale = lax.rsqrt(jnp.full((1, HALF), mean_of([a * a for a in apart]) + EPSILON, F32))
         keep.layer_norm = [a * keep.layer_scale for a in apart]
         keep.relu_image = jnp.concatenate([silu(a) for a in keep.layer_norm], axis=1).astype(BF16)
-        for copy in later[2:17]:
-            copy.wait_recv()
+        later[-1].wait_recv()
         keep.image_row = jnp.dot(
             jnp.broadcast_to(keep.relu_image, (16, FEAT)),
             proj[pl.ds(2 * FEAT, FEAT), pl.ds(lane, HALF)],
@@ -363,7 +380,7 @@
         )[0:1]
 
     _, (s0, s1, s2, s3) = totals(
-        0, [down(point), down(point * point), down(atrous), down(atrous * atrous)], (send_pools, image_forward)
+        0, [down(point), down(point * point), down(atrous), down(atrous * atrous)], (image_product, image_forward)
     )
     centre_p, scale_p = finish(s0, s1)
     centre_a, scale_a = finish(s2, s3)
@@ -392,6 +409,7 @@
     v.mixed[...] = mixed
 
     def slope_point():
+        send_pools()
         v.slope_p[...] = silu_slope(v.norm_p[...])
 
     def slope_atrous():
@@ -503,7 +521,7 @@
     v.grad_atrous[...] = grad_atrous.astype(BF16)
     upper = push(v.grad_atrous, v.back_halo.at[1], v.halo_send.at[2], v.halo_recv.at[2], z_peer(z, 2))
     lower = push(v.grad_atrous, v.back_halo.at[0], v.halo_send.at[3], v.halo_recv.at[3], z_peer(z, -2))
-    proj_copies = [
+    grad_copies = [
         push(
             v.proj_part.at[pl.ds(pl.multiple_of(lax.rem(sample + k, 16) * 48, 16), 48), :], v.proj_slots.at[sample],
             v.pgrad_send.at[k - 1], v.pgrad_recv.at[k - 1], sample_peer(sample, k),
@@ -512,12 +530,12 @@
     ]
     v.proj_slots[sample] = v.proj_part[own_rows, :]
     cols = v.cols
-    cols[:, pl.ds(0, HALF)] = back_norm(v.slope_p[...], v.norm_p[...], s0, s1, scale_p).astype(BF16)
+    cols[pl.ds(0, SPOTS), pl.ds(0, HALF)] = back_norm(v.slope_p[...], v.norm_p[...], s0, s1, scale_p).astype(BF16)
 
     def fill(r, source):
         for s in (-1, 0, 1):
             t = 1 + 3 * (r + 1) + (s + 1)
-            cols[:, pl.ds(t * HALF, HALF)] = moved(source, -RATE * s, column).astype(BF16)
+            cols[pl.ds(0, SPOTS), pl.ds(t * HALF, HALF)] = moved(source, -RATE * s, column).astype(BF16)
 
     fill(0, v.grad_atrous[...].astype(F32))
     upper.wait()
@@ -532,9 +550,7 @@
 
         def weight_part(k, carry):
             at = pl.ds(pl.multiple_of(base + k * FEAT, FEAT), FEAT)
-            part = lax.dot_general(
-                spots[:, at], cols[...], (((0,), (0,)), ((), ())), preferred_element_type=F32
-            )
+            part = jnp.dot(v.flipped[at, :], cols[...], preferred_element_type=F32)
             partial[at, :] = (part * FACTOR).astype(BF16)
             return carry
 
@@ -619,7 +635,7 @@
     def input_part(k, carry):
         at = pl.ds(pl.multiple_of(k * FEAT, FEAT), FEAT)
         part = lax.dot_general(
-            cols[...], full[at, pl.ds(0, WIDE)], (((1,), (1,)), ((), ())), preferred_element_type=F32
+            cols[pl.ds(0, SPOTS), :], full[at, pl.ds(0, WIDE)], (((1,), (1,)), ((), ())), preferred_element_type=F32
         )
         pool = lax.dot_general(
             grad_rows, full[at, pl.ds(WIDE, HALF)], (((1,), (1,)), ((), ())), preferred_element_type=F32
@@ -652,15 +668,15 @@
     for ring in last:
         ring.relay()
 
-    for copy in proj_copies:
+    for copy in grad_copies:
         copy.wait()
     v.proj_sum[...] = jnp.sum(v.proj_slots[...].astype(F32), axis=0).astype(BF16)
 
-    def to_strips(src, dst, send, recv):
-        return [push(src, dst, send.at[k - 1], recv.at[k - 1], strip_peer(strip, k)) for k in range(1, 16)]
-
-    spread = to_strips(v.proj_sum, v.proj_all.at[strip], v.spread_send, v.spread_recv)
-    v.proj_all[strip] = v.proj_sum[...]
+    def to_levels(src, dst, send, recv):
+        return [push(src, dst, send.at[k - 1], recv.at[k - 1], z_peer(z, k)) for k in range(1, 8)]
+
+    spread = to_levels(v.proj_sum, v.proj_all.at[z], v.spread_send, v.spread_recv)
+    v.proj_all[z] = v.proj_sum[...]
 
     for ring in last:
         ring.close()
@@ -685,7 +701,7 @@
     v.z_sum[...] = jnp.sum(v.z_slots[...].astype(F32), axis=0).astype(BF16)
     my_rows = pl.ds(pl.multiple_of(z * 16, 16), 16)
     joined = v.joined
-    all_copies = to_strips(v.z_sum, joined.at[c, my_rows, :], v.all_send, v.all_recv)
+    all_copies = to_levels(v.z_sum, joined.at[c, my_rows, :], v.all_send, v.all_recv)
     joined[c, my_rows, :] = v.z_sum[...]
 
     for copy in keep.pools + keep.images:
@@ -699,20 +715,41 @@
     )
     for copy in spread:
         copy.wait()
-    for k in range(2):
-        total = v.proj_all[k].astype(F32)
-        for level in range(1, 8):
-            total = total + v.proj_all[2 * level + k].astype(F32)
-        v.out_proj[:, pl.ds(k * HALF, HALF)] = total
+    v.proj_half[c] = jnp.sum(v.proj_all[...].astype(F32), axis=0)
+    swap_proj = swap(v.proj_half.at[c], v.proj_half.at[c], 9)
     for copy in ring_sent + later + done:
         copy.wait_send()
     keep.result.wait_send()
     for copy in all_copies:
         copy.wait()
+    swap_joined = swap(joined.at[c], joined.at[c], 10)
+
+    def store(k):
+        out = pl.ds(pl.multiple_of(k * HALF, HALF), HALF)
+        v.out_point[:, out] = joined[k, :, pl.ds(0, HALF)].astype(F32)
+        for t in range(9):
+            out = pl.ds(pl.multiple_of(t * FEAT + k * HALF, HALF), HALF)
+            v.out_atrous[:, out] = joined[k, :, pl.ds((t + 1) * HALF, HALF)].astype(F32)
+
+    store(c)
+    swap_proj.wait()
     for k in range(2):
-        v.out_point[:, pl.ds(k * HALF, HALF)] = joined[k, :, pl.ds(0, HALF)].astype(F32)
-        for t in range(9):
-            v.out_atrous[:, pl.ds(t * FEAT + k * HALF, HALF)] = joined[k, :, pl.ds((t + 1) * HALF, HALF)].astype(F32)
+        v.out_proj[:, pl.ds(k * HALF, HALF)] = v.proj_half[k]
+    swap_joined.wait()
+    store(1 - c)
+
+
+def finish_kernel(*refs):
+    ins, outs, rooms, (sems_in, sems_out) = refs[:6], refs[6:12], refs[12:18], refs[18:]
+    arriving = [pltpu.make_async_copy(ins[k], rooms[k], sems_in.at[k]) for k in range(6)]
+    leaving = [pltpu.make_async_copy(rooms[k], outs[k], sems_out.at[k]) for k in range(6)]
+    for copy in arriving:
+        copy.start()
+    for k in range(6):
+        arriving[k].wait()
+        leaving[k].start()
+    for copy in leaving:
+        copy.wait()
 
 
 VMEM = pl.BlockSpec(memory_space=pltpu.VMEM)
@@ -739,7 +776,8 @@
 SCRATCH = (
     ("stage", (ROWS, COLS, CHANS), BF16),
     ("cot_stage", (ROWS, COLS, FEAT), BF16),
-    ("spots", (SPOTS, CHANS), BF16),
+    ("spots", (DEPTH, CHANS), BF16),
+    ("flipped", (CHANS, DEPTH), BF16),
     ("full", (CHANS, WIDER), BF16),
     ("proj", (3 * FEAT, FEAT), BF16),
     ("taps", (TAPS, SPOTS, HALF), F32),
@@ -773,10 +811,11 @@
     ("proj_part", (3 * FEAT, HALF), BF16),
     ("proj_slots", (16, 48, HALF), BF16),
     ("proj_sum", (48, HALF), BF16),
-    ("proj_all", (16, 48, HALF), BF16),
+    ("proj_all", (8, 48, HALF), BF16),
+    ("proj_half", (2, 48, HALF), F32),
     ("grad_atrous", (SPOTS, HALF), BF16),
     ("back_halo", (2, SPOTS, HALF), BF16),
-    ("cols", (SPOTS, WIDE), BF16),
+    ("cols", (DEPTH, WIDE), BF16),
     ("partial", (CHANS, WIDE), BF16),
     ("opposite", (10, 2, 32, WIDE), BF16),
     ("beside", (10, 2, 64, WIDE), BF16),
@@ -790,7 +829,7 @@
 )
 SEMAPHORES = (
     ("local", (14,)),
-    ("core", (8,)),
+    ("core", (11,)),
     ("gather", (40,)),
     ("proj", (15,)),
     ("pool", (7,)),
@@ -802,8 +841,8 @@
     ("pgrad", (15,)),
     ("ring", (60,)),
     ("zsum", (7,)),
-    ("spread", (15,)),
-    ("all", (15,)),
+    ("spread", (7,)),
+    ("all", (7,)),
 )
 
 
@@ -826,6 +865,15 @@
         ),
         name="whole",
     )(images[0], w_point, w_atrous, w_image, w_proj, cotangent[0])
+    outs = pl.pallas_call(
+        finish_kernel,
+        out_shape=[shape for _, shape in OUTS],
+        in_specs=[ANY] * 6,
+        out_specs=[ANY] * 6,
+        scratch_shapes=[pltpu.VMEM(shape.shape, shape.dtype) for _, shape in OUTS] + [dma(6), dma(6)],
+        compiler_params=pltpu.CompilerParams(vmem_limit_bytes=60 << 20),
+        name="finish",
+    )(*outs)
     return (outs[0][None], outs[1][None], *outs[2:])
 
 

time: 184 us -> 165 us (0.90)
  Pallas kernels: 176 us -> 164 us
  local copies, waits for them, and re-layouts: 7.23 us -> 0 us
    pallas_call x1, Pallas kernels: 176 us -> 161 us  [on_device(): pl.pallas_call(functools.partial(whole_kernel, tuple(names)), out_shape=[...]
    unnamed x14 -> x0, local copies, waits for them, and re-layouts: 7.23 us -> none
    pallas_call x0 -> x1, Pallas kernels: none -> 3.1 us  [on_device(): pl.pallas_call(finish_kernel, out_shape=[shape for _, shape in OUTS], in_...]
where the time goes in v4:
time: 165 us
  Pallas kernels  164 us (99%)
    pallas_call x1, Pallas kernels, on_device(): pl.pallas_call(functools.partial(whole_kernel, tuple(names)), out_shape=[...  161 us

profile of v4, /device:TPU:1, one launch (start us, length us, event | category | flops | bytes accessed | tf_op | source)
XLA Modules:
  0.0 164.7 jit_solution(7523691056830308814)
XLA Ops:
  0.6 161.0 %whole.1 = (bf16[3,108,256]{2,1,0:T(8,128)(2,1)}, bf16[3,108,2048]{2,1,0:T(8,128)(2,1)}, f32[128,256]{1,0:T(8,128)}, f32[128,2304]{1,0:T(8,128)}, f32[128,256]{1,0:T(8,128)}, /*index=5*/f32[48,256]{1,0:T(8,128)}) custom-call(bf16[3,108,2048]{2,1,0:T(8,128)(2,1)} %bitcast.4, bf16[128,256]{1,0:T(8,128)(2,1)} %refs_1_.1, bf16[128,2304]{1,0:T(8,128)(2,1)} %refs_2_.1, ...), custom_call_target="tpu_custom_call" | custom-call | tf_op jit(solution)/shard_map/whole/pallas_call | solution.py:857
  161.6 3.1 %finish.1 = (bf16[3,108,256]{2,1,0:T(8,128)(2,1)}, bf16[3,108,2048]{2,1,0:T(8,128)(2,1)}, f32[128,256]{1,0:T(8,128)}, f32[128,2304]{1,0:T(8,128)}, f32[128,256]{1,0:T(8,128)}, /*index=5*/f32[48,256]{1,0:T(8,128)}) custom-call(bf16[3,108,256]{2,1,0:T(8,128)(2,1)} %get-tuple-element.18.refs_0_, bf16[3,108,2048]{2,1,0:T(8,128)(2,1)} %get-tuple-element.19.refs_1_, ...), custom_call_target="tpu_custom_call" | custom-call | tf_op jit(solution)/shard_map/finish/pallas_call | solution.py:868

commit v5 on v4

--- a/solution.py
+++ b/solution.py
@@ -94,7 +94,7 @@
     return jnp.where(inside, pltpu.roll(values, -offset, 0), 0.0)
 
 
-def ring_gather(full, y, x, send, recv, early, late):
+def ring_gather(full, y, x, send, recv, early, late, filler):
     count = [0]
     sent = []
 
@@ -148,9 +148,11 @@
         fr[kind].wait_recv()
         fl[kind].wait_recv()
         spread(kind, 2)
-    for a in (-1, 1, 2):
+        filler(kind)
+    for n, a in enumerate((-1, 1, 2)):
         for kind in kinds:
             relay(kind, a)
+            filler(2 + 2 * n + kind)
     for a in (0, -1, 1, 2):
         for kind in kinds:
             fu[kind, a].wait_recv()
@@ -248,14 +250,15 @@
         )
         v.pool_slots[z] = v.pool_src[...]
 
+    def filler(n):
         def flip(k, carry):
             at = pl.ds(pl.multiple_of(k * SHARD, SHARD), SHARD)
             v.flipped[at, :] = spots[:, at].T
             return carry
 
-        lax.fori_loop(0, CHANS // SHARD, flip, 0)
-
-    ring_sent = ring_gather(full, y, x, v.gather_send, v.gather_recv, early, late)
+        lax.fori_loop(2 * n, 2 * n + 2, flip, 0)
+
+    ring_sent = ring_gather(full, y, x, v.gather_send, v.gather_recv, early, late, filler)
 
     proj_copies = [
         push(
@@ -267,22 +270,24 @@
 
     def multiply(n, carry):
         product = jnp.dot(
-            spots[pl.ds(0, SPOTS), :], full[:, pl.ds(pl.multiple_of(n * FEAT, FEAT), FEAT)], preferred_element_type=F32
+            spots[pl.ds(0, SPOTS), :], full[:, pl.ds(n * FEAT if isinstance(n, int) else pl.multiple_of(n * FEAT, FEAT), FEAT)],
+            preferred_element_type=F32,
         )
         v.taps[2 * n] = product[:, :HALF]
         v.taps[2 * n + 1] = product[:, HALF:]
         return carry
 
-    lax.fori_loop(0, TAPS // 2, multiply, 0)
-
     def row_tap(r):
         first = 1 + 3 * (r + 1)
         return v.taps[first + 1] + moved(v.taps[first], -RATE, column) + moved(v.taps[first + 2], RATE, column)
 
+    lax.fori_loop(0, 2, multiply, 0)
     v.outer[0] = row_tap(-1).astype(BF16)
     below = push(v.outer.at[0], v.halo.at[0], v.halo_send.at[0], v.halo_recv.at[0], z_peer(z, 2))
+    lax.fori_loop(3, 5, multiply, 0)
     v.outer[1] = row_tap(1).astype(BF16)
     above = push(v.outer.at[1], v.halo.at[1], v.halo_send.at[1], v.halo_recv.at[1], z_peer(z, -2))
+    multiply(2, 0)
     v.centre[...] = row_tap(0)
     keep = types.SimpleNamespace()
 
@@ -408,7 +413,15 @@
     mixed = jnp.where(inside, mixed + mix_term(1 - c), 0.0)
     v.mixed[...] = mixed
 
+    def to_rows(source, slots, k):
+        return [
+            push(source, slots.at[1], v.halo_send.at[k], v.halo_recv.at[k], z_peer(z, 2)),
+            push(source, slots.at[0], v.halo_send.at[k + 1], v.halo_recv.at[k + 1], z_peer(z, -2)),
+        ]
+
     def slope_point():
+        v.norm_send[...] = v.norm_a[...].astype(BF16)
+        keep.norms = to_rows(v.norm_send, v.norm_halo, 2)
         send_pools()
         v.slope_p[...] = silu_slope(v.norm_p[...])
 
@@ -471,6 +484,8 @@
     v.slope_a[...] = up_atrous
 
     def image_backward():
+        v.up_send[...] = v.slope_a[...].astype(BF16)
+        keep.ups = to_rows(v.up_send, v.up_halo, 4)
         swap_columns.wait()
         column_b = jnp.concatenate([columns[0][0:1], columns[1][0:1]], axis=1).astype(BF16)
         back_image = lax.dot_general(
@@ -518,9 +533,6 @@
         return jnp.where(inside, grad, 0.0)
 
     grad_atrous = back_norm(v.slope_a[...], v.norm_a[...], s2, s3, scale_a)
-    v.grad_atrous[...] = grad_atrous.astype(BF16)
-    upper = push(v.grad_atrous, v.back_halo.at[1], v.halo_send.at[2], v.halo_recv.at[2], z_peer(z, 2))
-    lower = push(v.grad_atrous, v.back_halo.at[0], v.halo_send.at[3], v.halo_recv.at[3], z_peer(z, -2))
     grad_copies = [
         push(
             v.proj_part.at[pl.ds(pl.multiple_of(lax.rem(sample + k, 16) * 48, 16), 48), :], v.proj_slots.at[sample],
@@ -537,11 +549,15 @@
             t = 1 + 3 * (r + 1) + (s + 1)
             cols[pl.ds(0, SPOTS), pl.ds(t * HALF, HALF)] = moved(source, -RATE * s, column).astype(BF16)
 
-    fill(0, v.grad_atrous[...].astype(F32))
-    upper.wait()
-    fill(1, jnp.where(z >= 2, v.back_halo[1].astype(F32), zero))
-    lower.wait()
-    fill(-1, jnp.where(z < 6, v.back_halo[0].astype(F32), zero))
+    fill(0, grad_atrous)
+    for copy in keep.norms + keep.ups:
+        copy.wait()
+
+    def came_rows(k):
+        return back_norm(v.up_halo[k].astype(F32), v.norm_halo[k].astype(F32), s2, s3, scale_a)
+
+    fill(1, jnp.where(z >= 2, came_rows(1), zero))
+    fill(-1, jnp.where(z < 6, came_rows(0), zero))
 
     partial, opposite, beside = v.partial, v.opposite, v.beside
 
@@ -813,8 +829,10 @@
     ("proj_sum", (48, HALF), BF16),
     ("proj_all", (8, 48, HALF), BF16),
     ("proj_half", (2, 48, HALF), F32),
-    ("grad_atrous", (SPOTS, HALF), BF16),
-    ("back_halo", (2, SPOTS, HALF), BF16),
+    ("norm_send", (SPOTS, HALF), BF16),
+    ("norm_halo", (2, SPOTS, HALF), BF16),
+    ("up_send", (SPOTS, HALF), BF16),
+    ("up_halo", (2, SPOTS, HALF), BF16),
     ("cols", (DEPTH, WIDE), BF16),
     ("partial", (CHANS, WIDE), BF16),
     ("opposite", (10, 2, 32, WIDE), BF16),
@@ -835,7 +853,7 @@
     ("pool", (7,)),
     ("pall", (15,)),
     ("image", (15,)),
-    ("halo", (4,)),
+    ("halo", (6,)),
     ("z", (4, 7)),
     ("xy", (4, 15)),
     ("pgrad", (15,)),

time: 165 us -> 160 us (0.970)
  Pallas kernels: 164 us -> 159 us
    pallas_call x1, Pallas kernels: 161 us -> 156 us  [on_device(): pl.pallas_call(functools.partial(whole_kernel, tuple(names)), out_shape=[...]
where the time goes in v5:
time: 160 us
  Pallas kernels  159 us (99%)
    pallas_call x1, Pallas kernels, on_device(): pl.pallas_call(functools.partial(whole_kernel, tuple(names)), out_shape=[...  156 us

profile of v5, /device:TPU:1, one launch (start us, length us, event | category | flops | bytes accessed | tf_op | source)
XLA Modules:
  0.0 160.0 jit_solution(617724477534484582)
XLA Ops:
  0.6 156.1 %whole.1 = (bf16[3,108,256]{2,1,0:T(8,128)(2,1)}, bf16[3,108,2048]{2,1,0:T(8,128)(2,1)}, f32[128,256]{1,0:T(8,128)}, f32[128,2304]{1,0:T(8,128)}, f32[128,256]{1,0:T(8,128)}, /*index=5*/f32[48,256]{1,0:T(8,128)}) custom-call(bf16[3,108,2048]{2,1,0:T(8,128)(2,1)} %bitcast.4, bf16[128,256]{1,0:T(8,128)(2,1)} %refs_1_.1, bf16[128,2304]{1,0:T(8,128)(2,1)} %refs_2_.1, ...), custom_call_target="tpu_custom_call" | custom-call | tf_op jit(solution)/shard_map/whole/pallas_call | solution.py:875
  156.8 3.1 %finish.1 = (bf16[3,108,256]{2,1,0:T(8,128)(2,1)}, bf16[3,108,2048]{2,1,0:T(8,128)(2,1)}, f32[128,256]{1,0:T(8,128)}, f32[128,2304]{1,0:T(8,128)}, f32[128,256]{1,0:T(8,128)}, /*index=5*/f32[48,256]{1,0:T(8,128)}) custom-call(bf16[3,108,256]{2,1,0:T(8,128)(2,1)} %get-tuple-element.18.refs_0_, bf16[3,108,2048]{2,1,0:T(8,128)(2,1)} %get-tuple-element.19.refs_1_, ...), custom_call_target="tpu_custom_call" | custom-call | tf_op jit(solution)/shard_map/finish/pallas_call | solution.py:886

commit v6 on v5

--- a/solution.py
+++ b/solution.py
@@ -94,24 +94,35 @@
     return jnp.where(inside, pltpu.roll(values, -offset, 0), 0.0)
 
 
-def ring_gather(full, y, x, send, recv, early, late, filler):
-    count = [0]
-    sent = []
+def ring_gather(full, z, y, x, sems, early, late, filler):
+    send, recv, level_send, level_recv = sems
+    count = [0, 0]
+    sent, levels = [], []
+    odd = lax.rem(z, 2)
+    lanes = pl.ds(pl.multiple_of(odd * FEAT, FEAT), 4 * FEAT)
+    lent = pl.ds(pl.multiple_of(odd * 4 * FEAT, FEAT), FEAT)
+    partner = {"strip_0": z + 1 - 2 * odd}
+
+    def row_of(kind, a, b):
+        if kind == 0:
+            return lax.rem(y + b + 4, 4) * 4 + lax.rem(x + a + 4, 4)
+        return lax.rem(y + a + 4, 4) * 4 + lax.rem(x + b + 4, 4)
 
     def put(kind, a, b, part, first, d):
-        if kind == 0:
-            row = lax.rem(y + b + 4, 4) * 4 + lax.rem(x + a + 4, 4)
-            axis = "x" if first else "y"
-        else:
-            row = lax.rem(y + a + 4, 4) * 4 + lax.rem(x + b + 4, 4)
-            axis = "y" if first else "x"
+        axis = "x" if first == (kind == 0) else "y"
         start, size = ((0, 64), (0, 32), (32, 32))[part]
-        rows = pl.ds(pl.multiple_of(row * SHARD + kind * 64 + start, 32), size)
+        rows = pl.ds(pl.multiple_of(row_of(kind, a, b) * SHARD + kind * 64 + start, 32), size)
         k = count[0]
         count[0] += 1
-        copy = push(full.at[rows, :], full.at[rows, :], send.at[k], recv.at[k], along(axis, y, x, d))
+        copy = push(full.at[rows, lanes], full.at[rows, lanes], send.at[k], recv.at[k], along(axis, y, x, d))
         sent.append(copy)
         return copy
+
+    def lend(kind, a, b):
+        rows = pl.ds(pl.multiple_of(row_of(kind, a, b) * SHARD + kind * 64, 64), 64)
+        k = count[1]
+        count[1] += 1
+        levels.append(push(full.at[rows, lent], full.at[rows, lent], level_send.at[k], level_recv.at[k], partner))
 
     kinds = (0, 1)
     right, left, up, down = {}, {}, {}, {}
@@ -126,6 +137,14 @@
         fu[kind, a] = put(kind, a, -1, 1, False, 1)
         down[kind, a].wait_recv()
         fd[kind, a] = put(kind, a, 1, 2, False, -1)
+        lend(kind, a, -1)
+        lend(kind, a, 1)
+
+    def close(a):
+        for kind in kinds:
+            fu[kind, a].wait_recv()
+            fd[kind, a].wait_recv()
+            lend(kind, a, 2)
 
     for kind in kinds:
         right[kind] = put(kind, 0, 0, 0, True, 1)
@@ -141,6 +160,8 @@
     for kind in kinds:
         spread(kind, -1)
         spread(kind, 1)
+        lend(kind, -1, 0)
+        lend(kind, 1, 0)
     for kind in kinds:
         relay(kind, 0)
     late()
@@ -148,16 +169,17 @@
         fr[kind].wait_recv()
         fl[kind].wait_recv()
         spread(kind, 2)
+        lend(kind, 2, 0)
         filler(kind)
     for n, a in enumerate((-1, 1, 2)):
         for kind in kinds:
             relay(kind, a)
             filler(2 + 2 * n + kind)
-    for a in (0, -1, 1, 2):
-        for kind in kinds:
-            fu[kind, a].wait_recv()
-            fd[kind, a].wait_recv()
-    return sent
+        close((0, -1, 1)[n])
+    close(2)
+    for copy in levels:
+        copy.wait_recv()
+    return sent + levels
 
 
 def silu(v):
@@ -258,7 +280,13 @@
 
         lax.fori_loop(2 * n, 2 * n + 2, flip, 0)
 
-    ring_sent = ring_gather(full, y, x, v.gather_send, v.gather_recv, early, late, filler)
+    ring_sems = (v.gather_send, v.gather_recv, v.level_send, v.level_recv)
+    ring_sent = ring_gather(full, z, y, x, ring_sems, early, late, filler)
+    image_part = full.at[shard, pl.ds(WIDE, HALF)]
+    image_copies = [
+        push(image_part, image_part, v.wimage_send.at[k - 1], v.wimage_recv.at[k - 1], sample_peer(sample, k))
+        for k in range(1, 16)
+    ]
 
     proj_copies = [
         push(
@@ -357,7 +385,7 @@
         v.pool_all[sample] = v.pool_rows[sample]
 
     def image_product():
-        for copy in pools:
+        for copy in pools + image_copies:
             copy.wait()
         keep.pooled = (jnp.sum(v.pool_slots[...], axis=0) / SAMPLE_AREA).astype(BF16)
         image = jnp.dot(
@@ -849,6 +877,8 @@
     ("local", (14,)),
     ("core", (11,)),
     ("gather", (40,)),
+    ("level", (30,)),
+    ("wimage", (15,)),
     ("proj", (15,)),
     ("pool", (7,)),
     ("pall", (15,)),

time: 160 us -> 158 us (0.988)
  Pallas kernels: 159 us -> 157 us
    pallas_call x1, Pallas kernels: 156 us -> 154 us  [on_device(): pl.pallas_call(functools.partial(whole_kernel, tuple(names)), out_shape=[...]
where the time goes in v6:
time: 158 us
  Pallas kernels  157 us (99%)
    pallas_call x1, Pallas kernels, on_device(): pl.pallas_call(functools.partial(whole_kernel, tuple(names)), out_shape=[...  154 us

profile of v6, /device:TPU:1, one launch (start us, length us, event | category | flops | bytes accessed | tf_op | source)
XLA Modules:
  0.0 158.2 jit_solution(9945196136277608204)
XLA Ops:
  0.6 154.3 %whole.1 = (bf16[3,108,256]{2,1,0:T(8,128)(2,1)}, bf16[3,108,2048]{2,1,0:T(8,128)(2,1)}, f32[128,256]{1,0:T(8,128)}, f32[128,2304]{1,0:T(8,128)}, f32[128,256]{1,0:T(8,128)}, /*index=5*/f32[48,256]{1,0:T(8,128)}) custom-call(bf16[3,108,2048]{2,1,0:T(8,128)(2,1)} %bitcast.4, bf16[128,256]{1,0:T(8,128)(2,1)} %refs_1_.1, bf16[128,2304]{1,0:T(8,128)(2,1)} %refs_2_.1, ...), custom_call_target="tpu_custom_call" | custom-call | tf_op jit(solution)/shard_map/whole/pallas_call | solution.py:905
  154.9 3.1 %finish.1 = (bf16[3,108,256]{2,1,0:T(8,128)(2,1)}, bf16[3,108,2048]{2,1,0:T(8,128)(2,1)}, f32[128,256]{1,0:T(8,128)}, f32[128,2304]{1,0:T(8,128)}, f32[128,256]{1,0:T(8,128)}, /*index=5*/f32[48,256]{1,0:T(8,128)}) custom-call(bf16[3,108,256]{2,1,0:T(8,128)(2,1)} %get-tuple-element.18.refs_0_, bf16[3,108,2048]{2,1,0:T(8,128)(2,1)} %get-tuple-element.19.refs_1_, ...), custom_call_target="tpu_custom_call" | custom-call | tf_op jit(solution)/shard_map/finish/pallas_call | solution.py:916
